TPU v7x, 512 devices: a whole 4x4x16 slice. The times are simulated.
512 devices in a mesh: depth: 8 (over y, core), tile: 16 (over z), brick: 4 (over x).
Axes of the slice: x: 4, y: 4, z: 16, core: 2. Of those that a mesh axis runs over, the one named last changes fastest.
Arguments:
- fragments: float32 [8, 64, 64, 2, 16, 128], P('depth', ('tile', 'brick')), may hold values from 0 to 0.61, as said below
- layer_rank: int32 [8, 64, 64, 2, 4, 128], P('depth', ('tile', 'brick')), may hold values from 0 to 3, as said below
- pixel_count: int32 [8, 64, 64, 2], P('depth', ('tile', 'brick')), may hold values from 1 to 128
- slot_count: int32 [8, 64, 64], P('depth', ('tile', 'brick')), may hold values from 0 to 2, as said below
- block_run: int32 [8, 64, 64, 2], P('depth', ('tile', 'brick')), may hold values from 0 to 255, as said below
- brick_order: int32 [8, 64], P('depth'), may hold values from 0 to 63, each once within a row
- interlace: int32 [256], replicated, may hold values from 0 to 255, as said below
Outputs:
- image: float32 [64, 8, 32, 4, 128], P(('tile', 'brick'), 'depth')
Inputs may be any that keep to these rules, and one draw needn't show every extreme that they name: `fragments`: each entry is r, g, b, alpha with alpha at least 0.003 and each color between 0 and alpha. `layer_rank`: at every pixel the four ranks are 0, 1, 2 and 3 in some order. `slot_count`: in every slab some owner receives 2 live blocks from every brick. `block_run`: the slots that one brick sends to one owner name distinct strip slots. `brick_order`: each slab's ranks name every brick once. `interlace`: each value once; every aligned group of 32 consecutive entries holds exactly 4 values of each aligned range of 32 values.
All inputs are finite; a program needn't handle non-finite values.
Results may differ from a plain program's by a relative error of at most 0.0003.
Values sent between devices are 32-bit elements; how exact they have to be, the bound alone decides.
No kernel may reach another device: no remote copies, remote signals or barrier semaphores. Data moves between devices by JAX's collectives and lax.ppermute only.
A program may use at most 64 MiB of HBM per device.

v0:
```python
import jax
import jax.numpy as jnp
from jax import lax
from jax.sharding import PartitionSpec as P


def swapped(block, axis, bit):
    count = lax.axis_size(axis)
    route = []
    for low in range(count):
        high = low | 1 << bit
        if high != low and high < count:
            route += [(low, high), (high, low)]
    return lax.ppermute(block, axis, route)


def order_layers(layers, ranks, counts):
    width = layers.shape[-1]
    pixel = lax.broadcasted_iota(jnp.int32, counts.shape + (width,), 2)
    visible = (pixel < counts[:, :, None]).astype(jnp.float32)
    placed = []
    for position in range(4):
        chosen = jnp.zeros(layers.shape[:2] + layers.shape[3:], jnp.float32)
        for layer in range(4):
            picked = (ranks[:, :, layer, :] == position).astype(jnp.float32)
            chosen = chosen + picked[:, :, None, :] * layers[:, :, layer]
        placed.append(chosen * visible[:, :, None, :])
    return jnp.stack(placed, axis=2)


def blend(layers):
    result = layers[..., 3, :, :]
    for position in (2, 1, 0):
        front = layers[..., position, :, :]
        result = front + (1.0 - front[..., 3:4, :]) * result
    return result


def over(front, back):
    return front + (1.0 - front[..., 3:4, :]) * back


def compose_strip(blocks, live, runs, brick_rank, slots):
    keeping = jnp.log(1.0 - blocks[:, 3, :] * live[:, None])
    same = runs[:, None] == runs[None, :]
    before = brick_rank[None, :] < brick_rank[:, None]
    earlier = (same & before).astype(jnp.float32)
    passed = jnp.exp(jnp.dot(earlier, keeping, precision=lax.Precision.HIGHEST))
    shaded = (blocks * live[:, None, None] * passed[:, None, :]).reshape(
        blocks.shape[0], 4 * blocks.shape[-1]
    )
    target = (lax.broadcasted_iota(jnp.int32, (slots, runs.shape[0]), 0) == runs[None, :]).astype(
        jnp.float32
    )
    strip = jnp.dot(target, shaded, precision=lax.Precision.HIGHEST)
    return strip.reshape(slots, 4, blocks.shape[-1])


def deliver(outgoing):
    return lax.all_to_all(outgoing, ("tile", "brick"), split_axis=0, concat_axis=0, tiled=True)


def shards(fragments, layer_rank, pixel_count, slot_count, block_run, brick_order, interlace):
    owners = fragments.shape[2]
    capacity = fragments.shape[3]
    width = fragments.shape[-1]
    slots = interlace.shape[0]
    layers = fragments.reshape(owners, capacity, 4, 4, width)
    ordered = order_layers(
        layers,
        layer_rank.reshape(owners, capacity, 4, width),
        pixel_count.reshape(owners, capacity),
    )
    blocks = deliver(blend(ordered))
    blocks = blocks.reshape(owners * capacity, 4, width)
    live = (
        (lax.broadcasted_iota(jnp.int32, (owners, capacity), 1) < slot_count.reshape(owners, 1))
        .astype(jnp.float32)
        .reshape(owners * capacity)
    )
    runs = block_run.reshape(owners * capacity)
    brick_rank = jnp.repeat(brick_order.reshape(owners), capacity)
    strip = compose_strip(blocks, live, runs, brick_rank, slots)
    depth_count = lax.axis_size("depth")
    depth_bits = depth_count.bit_length() - 1
    place = lax.axis_index("depth")
    share = slots // depth_count
    mine = strip
    for bit in range(depth_bits):
        half = mine.shape[0] // 2
        lower = mine[:half]
        upper = mine[half:]
        first = place >> bit & 1 == 0
        kept = jnp.where(first, lower, upper)
        sent = jnp.where(first, upper, lower)
        partner = swapped(sent, "depth", bit)
        mine = jnp.where(first, over(kept, partner), over(partner, kept))
    per_tile = share // depth_count
    device_ids = lax.broadcasted_iota(jnp.int32, (depth_count,), 0)
    offsets = jnp.zeros((depth_count,), jnp.int32)
    for bit in range(depth_bits):
        offsets = offsets + (device_ids >> bit & 1) * (slots >> bit + 1)
    along = lax.broadcasted_iota(jnp.int32, (share,), 0)
    screen = jnp.take(interlace, offsets[:, None] + along[None, :], axis=0)
    tile_of = screen // share
    own_tile = jnp.take(tile_of, place, axis=0)
    earlier_same = (own_tile[None, :] == own_tile[:, None]) & (along[None, :] < along[:, None])
    slot_of = own_tile * per_tile + jnp.sum(earlier_same.astype(jnp.int32), axis=1)
    source_row = jnp.sum(jnp.where(slot_of[None, :] == along[:, None], along[None, :], 0), axis=1)
    outgoing = jnp.take(mine, source_row, axis=0).reshape(depth_count, per_tile, 4, width)
    incoming = lax.all_to_all(outgoing, "depth", split_axis=0, concat_axis=0, tiled=True).reshape(
        share, 4, width
    )
    mine_mask = tile_of == place
    counted = jnp.cumsum(mine_mask.astype(jnp.int32), axis=1) - 1
    rank_ids = lax.broadcasted_iota(jnp.int32, (depth_count, per_tile, share), 1)
    selected = mine_mask[:, None, :] & (counted[:, None, :] == rank_ids)
    local_place = jnp.sum(
        jnp.where(selected, screen[:, None, :] - place * share, 0), axis=2
    ).reshape(share)
    pick = jnp.sum(jnp.where(local_place[None, :] == along[:, None], along[None, :], 0), axis=1)
    result = jnp.take(incoming, pick, axis=0)
    return result.reshape(1, 1, share, 4, width)


def solution(mesh):
    return jax.shard_map(
        shards,
        mesh=mesh,
        in_specs=(
            P("depth", ("tile", "brick"), None, None, None, None),
            P("depth", ("tile", "brick"), None, None, None, None),
            P("depth", ("tile", "brick"), None, None),
            P("depth", ("tile", "brick"), None),
            P("depth", ("tile", "brick"), None, None),
            P("depth", None),
            P(),
        ),
        out_specs=P(("tile", "brick"), "depth", None, None, None),
        check_vma=False,
    )
```

profile of v0, /device:TPU:1, one launch (start us, length us, event | category | flops | bytes accessed | tf_op | source)
XLA Modules:
  0.0 80.1 jit_solution(10792739169343043280)
XLA Ops:
  0.0 2.5 %compare_convert_fusion.3 = (f32[64,2,1,128]{3,2,1,0:T(1,128)S(1)}, f32[64,2,1,128]{3,2,1,0:T(1,128)S(1)}, f32[64,2,1,128]{3,2,1,0:T(1,128)S(1)}, f32[64,2,1,128...) fusion(s32[64,2,4,128]{3,2,1,0:T(4,128)} %bitcast.123), kind=kLoop, calls=%fused_computation.21 | loop fusion | flops 524288 | bytes 1310720 | tf_op jit(solution)/shard_map/mul | solution.py:26
  2.6 0.7 copy-done.2
  3.8 0.3 add_multiply_fusion
  4.3 1.2 %multiply_add_fusion = f32[64,2,4,128]{3,2,1,0:T(4,128)} fusion(f32[64,2,4,128]{3,2,1,0:T(4,128)S(1)} %get-tuple-element.21, f32[64,2,4,128]{3,2,1,0:T(4,128)S(1)} %get-tuple-element.20, f32[64,2,4,4,128]{4,3,2,1,0:T(4,128)S(1)} %bitcast.111, f32[64,2,128]{2,1,0:T(2,128)S(1)} %bitcast.127, f32[64,2,128]{2,1,0:T(2,128)S(1)} %bitcast.126, ...), kind=kLoop, calls=%fused_computation.14 | loop fusion | flops 1441792 | bytes 2621440 | tf_op jit(solution)/shard_map/add | solution.py:35
  5.5 19.1 %all-to-all-start = ((f32[64,2,4,128]{3,2,1,0:T(4,128)}), f32[64,2,4,128]{3,2,1,0:T(4,128)S(1)}, u32[]{:S(2)}, u32[]{:S(2)}) async-start(f32[64,2,4,128]{3,2,1,0:T(4,128)} %multiply_add_fusion), calls=%async_computation | async-start | bytes 524288 | tf_op jit(solution)/shard_map/all_to_all | solution.py:60
  24.7 0.6 copy-done.4
  25.6 1.9 %gather_fusion = s32[256]{0:T(256)S(1)} fusion(s32[256]{0:T(256)S(1)} %copy-done, s32[1024]{0:T(1024)S(1)} %pad_clamp_fusion.2), kind=kCustom, calls=%fused_computation.2 | custom fusion | bytes 3072 | tf_op jit(solution)/shard_map/jit(_take)/gather | solution.py:104
  28.4 0.7 copy-done.3
  29.5 0.6 copy-done.5
  30.7 13.1 %all-to-all-done = f32[64,2,4,128]{3,2,1,0:T(4,128)S(1)} async-done(((f32[64,2,4,128]{3,2,1,0:T(4,128)}), f32[64,2,4,128]{3,2,1,0:T(4,128)S(1)}, u32[]{:S(2)}, u32[]{:S(2)}) %all-to-all-start) | async-done | bytes 262176 | tf_op jit(solution)/shard_map/all_to_all | solution.py:60
  43.9 0.3 convolution_exponential_fusion
  44.3 0.5 fusion
  44.9 6.1 %collective-permute-start = (f32[128,4,128]{2,1,0:T(4,128)S(1)}, f32[128,4,128]{2,1,0:T(4,128)S(1)}, u32[]{:S(2)}, u32[]{:S(2)}) collective-permute-start(f32[128,4,128]{2,1,0:T(4,128)S(1)} %select_n.155), channel_id=1, source_target_pairs={{0,64},{64,0},{128,192},{192,128},{256,320},{320,256},{384,448},{4... | collective-permute-start | bytes 786440 | tf_op jit(solution)/shard_map/ppermute | solution.py:14
  51.2 0.9 %collective-permute-done = f32[128,4,128]{2,1,0:T(4,128)S(1)} collective-permute-done((f32[128,4,128]{2,1,0:T(4,128)S(1)}, f32[128,4,128]{2,1,0:T(4,128)S(1)}, u32[]{:S(2)}, u32[]{:S(2)}) %collective-permute-start) | collective-permute-done | bytes 262176 | tf_op jit(solution)/shard_map/ppermute | solution.py:14
  52.4 3.2 %collective-permute-start.1 = (f32[64,4,128]{2,1,0:T(4,128)S(1)}, f32[64,4,128]{2,1,0:T(4,128)S(1)}, u32[]{:S(2)}, u32[]{:S(2)}) collective-permute-start(f32[64,4,128]{2,1,0:T(4,128)S(1)} %get-tuple-element.25), channel_id=1, source_target_pairs={{0,128},{128,0},{64,192},{192,64},{256,384},{384,256},{320,448},{4... | collective-permute-start | bytes 393224 | tf_op jit(solution)/shard_map/ppermute | solution.py:14
  55.7 3.3 %collective-permute-done.1 = f32[64,4,128]{2,1,0:T(4,128)S(1)} collective-permute-done((f32[64,4,128]{2,1,0:T(4,128)S(1)}, f32[64,4,128]{2,1,0:T(4,128)S(1)}, u32[]{:S(2)}, u32[]{:S(2)}) %collective-permute-start.1) | collective-permute-done | bytes 131104 | tf_op jit(solution)/shard_map/ppermute | solution.py:14
  59.2 4.8 %collective-permute-start.2 = (f32[32,4,128]{2,1,0:T(4,128)S(1)}, f32[32,4,128]{2,1,0:T(4,128)S(1)}, u32[]{:S(2)}, u32[]{:S(2)}) collective-permute-start(f32[32,4,128]{2,1,0:T(4,128)S(1)} %get-tuple-element.43), channel_id=1, source_target_pairs={{0,256},{256,0},{64,320},{320,64},{128,384},{384,128},{192,448},{4... | collective-permute-start | bytes 196616 | tf_op jit(solution)/shard_map/ppermute | solution.py:14
  64.0 1.7 %collective-permute-done.2 = f32[32,4,128]{2,1,0:T(4,128)S(1)} collective-permute-done((f32[32,4,128]{2,1,0:T(4,128)S(1)}, f32[32,4,128]{2,1,0:T(4,128)S(1)}, u32[]{:S(2)}, u32[]{:S(2)}) %collective-permute-start.2) | collective-permute-done | bytes 65568 | tf_op jit(solution)/shard_map/ppermute | solution.py:14
  65.8 0.6 gather_fusion.1
  66.4 0.7 broadcast_select_fusion
  67.1 6.8 %all-to-all-start.1 = ((f32[8,4,4,128]{3,2,1,0:T(4,128)}), f32[8,4,4,128]{3,2,1,0:T(4,128)S(1)}, u32[]{:S(2)}, u32[]{:S(2)}) async-start(f32[8,4,4,128]{3,2,1,0:T(4,128)} %bitcast.37), calls=%async_computation.1 | async-start | bytes 131072 | tf_op jit(solution)/shard_map/all_to_all | solution.py:111
  73.9 4.8 %all-to-all-done.1 = f32[8,4,4,128]{3,2,1,0:T(4,128)S(1)} async-done(((f32[8,4,4,128]{3,2,1,0:T(4,128)}), f32[8,4,4,128]{3,2,1,0:T(4,128)S(1)}, u32[]{:S(2)}, u32[]{:S(2)}) %all-to-all-start.1) | async-done | bytes 65568 | tf_op jit(solution)/shard_map/all_to_all | solution.py:111
  78.8 0.6 gather_fusion.2
  79.4 0.7 select_bitcast_fusion
  (58 shorter events, 3.7 us)
Async XLA Ops:
  0.0 25.6 %copy-start = (s32[256]{0:T(256)S(1)}, s32[256]{0:T(256)}, u32[]{:S(2)}) copy-start(s32[256]{0:T(256)} %param.15) | copy-start | bytes 3076
  0.0 3.5 %copy-start.1 = (f32[1,1,64,2,16,128]{5,4,3,2,1,0:T(8,128)S(1)}, f32[1,1,64,2,16,128]{5,4,3,2,1,0:T(8,128)}, u32[]{:S(2)}) copy-start(f32[1,1,64,2,16,128]{5,4,3,2,1,0:T(8,128)} %param.9) | copy-start | bytes 3145732
  2.6 0.7 copy-start.2
  5.5 38.3 %all-to-all-start = ((f32[64,2,4,128]{3,2,1,0:T(4,128)}), f32[64,2,4,128]{3,2,1,0:T(4,128)S(1)}, u32[]{:S(2)}, u32[]{:S(2)}) async-start(f32[64,2,4,128]{3,2,1,0:T(4,128)} %multiply_add_fusion), calls=%async_computation | async-start | bytes 524288 | tf_op jit(solution)/shard_map/all_to_all | solution.py:60
  24.7 0.7 copy-start.4
  28.4 0.7 copy-start.3
  29.5 0.7 copy-start.5
  44.9 7.3 %collective-permute-start = (f32[128,4,128]{2,1,0:T(4,128)S(1)}, f32[128,4,128]{2,1,0:T(4,128)S(1)}, u32[]{:S(2)}, u32[]{:S(2)}) collective-permute-start(f32[128,4,128]{2,1,0:T(4,128)S(1)} %select_n.155), channel_id=1, source_target_pairs={{0,64},{64,0},{128,192},{192,128},{256,320},{320,256},{384,448},{4... | collective-permute-start | bytes 786440 | tf_op jit(solution)/shard_map/ppermute | solution.py:14
  52.4 6.6 %collective-permute-start.1 = (f32[64,4,128]{2,1,0:T(4,128)S(1)}, f32[64,4,128]{2,1,0:T(4,128)S(1)}, u32[]{:S(2)}, u32[]{:S(2)}) collective-permute-start(f32[64,4,128]{2,1,0:T(4,128)S(1)} %get-tuple-element.25), channel_id=1, source_target_pairs={{0,128},{128,0},{64,192},{192,64},{256,384},{384,256},{320,448},{4... | collective-permute-start | bytes 393224 | tf_op jit(solution)/shard_map/ppermute | solution.py:14
  59.2 6.5 %collective-permute-start.2 = (f32[32,4,128]{2,1,0:T(4,128)S(1)}, f32[32,4,128]{2,1,0:T(4,128)S(1)}, u32[]{:S(2)}, u32[]{:S(2)}) collective-permute-start(f32[32,4,128]{2,1,0:T(4,128)S(1)} %get-tuple-element.43), channel_id=1, source_target_pairs={{0,256},{256,0},{64,320},{320,64},{128,384},{384,128},{192,448},{4... | collective-permute-start | bytes 196616 | tf_op jit(solution)/shard_map/ppermute | solution.py:14
  67.1 11.7 %all-to-all-start.1 = ((f32[8,4,4,128]{3,2,1,0:T(4,128)}), f32[8,4,4,128]{3,2,1,0:T(4,128)S(1)}, u32[]{:S(2)}, u32[]{:S(2)}) async-start(f32[8,4,4,128]{3,2,1,0:T(4,128)} %bitcast.37), calls=%async_computation.1 | async-start | bytes 131072 | tf_op jit(solution)/shard_map/all_to_all | solution.py:111
where the time goes:
time: 80.5 us; the launch traced here: 80.1 us
  starting transfers between devices  40.1 us (50%)
  waiting for transfers between devices  23.9 us (30%)
  other arithmetic  7.91 us (10%)
  local copies, waits for them, and re-layouts  7.13 us (9%)
    all_to_all x1, starting transfers between devices, deliver(): lax.all_to_all(outgoing, ('tile', 'brick'), split_axis=0, concat_axis=0,...  19.1 us
    ppermute x3, starting transfers between devices, swapped(): return lax.ppermute(block, axis, route)  14.1 us
    all_to_all x1, waiting for transfers between devices, deliver(): lax.all_to_all(outgoing, ('tile', 'brick'), split_axis=0, concat_axis=0,...  13.1 us
    all_to_all x1, starting transfers between devices, shards(): lax.all_to_all(outgoing, 'depth', split_axis=0, concat_axis=0, tiled=True)  6.82 us
    ppermute x3, waiting for transfers between devices, swapped(): return lax.ppermute(block, axis, route)  5.92 us
    all_to_all x1, waiting for transfers between devices, shards(): lax.all_to_all(outgoing, 'depth', split_axis=0, concat_axis=0, tiled=True)  4.84 us
    unnamed x13, local copies, waits for them, and re-layouts  2.76 us
    mul x1, other arithmetic, order_layers(): chosen = chosen + picked[:, :, None, :] * layers[:, :, layer]  2.54 us
  transfers between devices with their start and end apart: 5, of which 5 were waited for; matrix products, arithmetic and copies ran while one was open for 5% of the time, Pallas kernels for 0%

commit v1 on v0

v1 whole, which is shorter than its diff:
```python
import jax
import jax.numpy as jnp
from jax import lax
from jax.experimental import pallas as pl
from jax.experimental.pallas import tpu as pltpu
from jax.sharding import PartitionSpec as P


def columns(row, first, rows, width):
    length = row.shape[1]
    place = lax.broadcasted_iota(jnp.int32, (rows, length), 1)
    own = lax.broadcasted_iota(jnp.int32, (rows, length), 0) + first
    spread = jnp.where(place == own, row.astype(jnp.float32), 0.0).astype(jnp.bfloat16)
    return jnp.dot(
        spread, jnp.ones((length, width), jnp.bfloat16), preferred_element_type=jnp.float32
    )


def halves(values):
    high = values.astype(jnp.bfloat16)
    low = (values - high.astype(jnp.float32)).astype(jnp.bfloat16)
    return high, low


def blend_kernel(capacity, fragments, ranks, counts, out):
    owners = out.shape[0] // (capacity * 4)
    width = out.shape[1]
    first = pl.program_id(0) * owners
    pixel = lax.broadcasted_iota(jnp.int32, (owners, width), 1).astype(jnp.float32)
    for slot in range(capacity):
        visible = pixel < columns(counts[slot : slot + 1, :], first, owners, width)
        rank = [ranks[pl.ds(slot * 4 + layer, owners, stride=capacity * 4), :] for layer in range(4)]
        entry = [
            [
                fragments[pl.ds(slot * 16 + layer * 4 + part, owners, stride=capacity * 16), :]
                for part in range(4)
            ]
            for layer in range(4)
        ]
        clear = [1.0 - entry[layer][3] for layer in range(4)]
        weight = [jnp.where(visible, 1.0, 0.0)] * 4
        for one in range(4):
            for two in range(one + 1, 4):
                ahead = rank[one] < rank[two]
                weight[two] = weight[two] * jnp.where(ahead, clear[one], 1.0)
                weight[one] = weight[one] * jnp.where(ahead, 1.0, clear[two])
        for part in range(4):
            mixed = entry[0][part] * weight[0]
            for layer in range(1, 4):
                mixed = mixed + entry[layer][part] * weight[layer]
            out[pl.ds(slot * 4 + part, owners, stride=capacity * 4), :] = mixed


def blend(fragments, ranks, counts, steps):
    owners, capacity, _, width = fragments.shape
    flat = fragments.reshape(owners * capacity * 16, width)
    flat_ranks = ranks.reshape(owners * capacity * 4, width)
    rows = owners * capacity // steps

    def kernel(*refs):
        blend_kernel(capacity, *refs)

    return pl.pallas_call(
        kernel,
        grid=(steps,),
        in_specs=[
            pl.BlockSpec((rows * 16, width), lambda i: (i, 0)),
            pl.BlockSpec((rows * 4, width), lambda i: (i, 0)),
            pl.BlockSpec((capacity, owners), lambda i: (0, 0)),
        ],
        out_specs=pl.BlockSpec((rows * 4, width), lambda i: (i, 0)),
        out_shape=jax.ShapeDtypeStruct((owners * capacity * 4, width), jnp.float32),
        name="blend",
    )(flat, flat_ranks, counts)


def plan_kernel(counts, runs, order, interlace, earlier, target):
    capacity, bricks = runs.shape
    slots = interlace.shape[1]
    total = capacity * bricks
    run = jnp.concatenate([runs[slot : slot + 1, :] for slot in range(capacity)], axis=1)
    rank = jnp.concatenate([order[...]] * capacity, axis=1)
    live = jnp.concatenate([jnp.where(counts[...] > slot, 1, 0) for slot in range(capacity)], axis=1) > 0
    run_of = columns(run, 0, total, total).astype(jnp.int32)
    rank_of = columns(rank, 0, total, total).astype(jnp.int32)
    ahead = (run_of == run) & (rank < rank_of) & live
    earlier[...] = jnp.where(ahead, 1.0, 0.0).astype(jnp.bfloat16)
    slot_id = lax.broadcasted_iota(jnp.int32, (slots, total), 0)
    landing = jnp.where(slot_id == run, 1.0, 0.0).astype(jnp.bfloat16)
    screen = jnp.dot(
        jnp.broadcast_to(interlace[...].astype(jnp.float32), (8, slots)).astype(jnp.bfloat16),
        landing,
        preferred_element_type=jnp.float32,
    )[0:1, :].astype(jnp.int32)
    target[...] = jnp.where((slot_id == screen) & live, 1.0, 0.0).astype(jnp.bfloat16)


def plan(counts, runs, order, interlace):
    capacity, bricks = runs.shape
    total = capacity * bricks
    slots = interlace.shape[1]
    return pl.pallas_call(
        plan_kernel,
        out_shape=(
            jax.ShapeDtypeStruct((total, total), jnp.bfloat16),
            jax.ShapeDtypeStruct((slots, total), jnp.bfloat16),
        ),
        name="plan",
    )(counts, runs, order, interlace)


def strip_kernel(capacity, blocks, earlier, target, out):
    bricks = blocks.shape[0] // (capacity * 4)
    tiles, _, share, width = out.shape

    def part_of(part):
        return jnp.concatenate(
            [blocks[pl.ds(slot * 4 + part, bricks, stride=capacity * 4), :] for slot in range(capacity)],
            axis=0,
        )

    def picked(matrix, values):
        high, low = halves(values)
        return jnp.dot(matrix, high, preferred_element_type=jnp.float32) + jnp.dot(
            matrix, low, preferred_element_type=jnp.float32
        )

    alpha = part_of(3)
    passed = jnp.exp(picked(earlier[...], jnp.log(1.0 - alpha)))
    shaded = jnp.concatenate([part_of(0) * passed, part_of(1) * passed, part_of(2) * passed, alpha * passed], axis=1)
    strip = picked(target[...], shaded)
    for tile in range(tiles):
        for part in range(4):
            out[tile, part] = strip[tile * share : (tile + 1) * share, part * width : (part + 1) * width]


def compose_strip(blocks, earlier, target, capacity, tiles):
    width = blocks.shape[1]
    slots = target.shape[0]

    def kernel(*refs):
        strip_kernel(capacity, *refs)

    return pl.pallas_call(
        kernel,
        out_shape=jax.ShapeDtypeStruct((tiles, 4, slots // tiles, width), jnp.float32),
        name="strip",
    )(blocks, earlier, target)


def stack_kernel(strips, out):
    slabs, _, share, _ = strips.shape
    total = [strips[slabs - 1, part] for part in range(4)]
    for slab in range(slabs - 2, -1, -1):
        clear = 1.0 - strips[slab, 3]
        total = [strips[slab, part] + clear * total[part] for part in range(4)]
    for part in range(4):
        out[pl.ds(part, share, stride=4), :] = total[part]


def stack(strips):
    _, _, share, width = strips.shape
    return pl.pallas_call(
        stack_kernel,
        out_shape=jax.ShapeDtypeStruct((share * 4, width), jnp.float32),
        name="stack",
    )(strips)


def shards(fragments, layer_rank, pixel_count, slot_count, block_run, brick_order, interlace):
    _, _, owners, capacity, _, width = fragments.shape
    slots = interlace.shape[0]
    tiles = lax.axis_size("depth")
    blocks = blend(
        fragments[0, 0],
        layer_rank[0, 0],
        pixel_count[0, 0].T,
        4,
    )
    sent = lax.all_to_all(
        blocks.reshape(owners, capacity * 4, width), ("tile", "brick"), split_axis=0, concat_axis=0, tiled=True
    )
    earlier, target = plan(slot_count[0], block_run[0, 0].T, brick_order, interlace.reshape(1, slots))
    strip = compose_strip(sent.reshape(owners * capacity * 4, width), earlier, target, capacity, tiles)
    strips = lax.all_to_all(strip, "depth", split_axis=0, concat_axis=0, tiled=True)
    return stack(strips).reshape(1, 1, slots // tiles, 4, width)


def solution(mesh):
    return jax.shard_map(
        shards,
        mesh=mesh,
        in_specs=(
            P("depth", ("tile", "brick"), None, None, None, None),
            P("depth", ("tile", "brick"), None, None, None),
            P("depth", ("tile", "brick"), None, None),
            P("depth", ("tile", "brick"), None),
            P("depth", ("tile", "brick"), None, None),
            P("depth", None),
            P(),
        ),
        out_specs=P(("tile", "brick"), "depth", None, None, None),
        check_vma=False,
    )
```

time: 80.5 us -> 65.1 us (0.81)
  starting transfers between devices: 40.1 us -> 19.1 us
  blocking collectives: 0 us -> 18.1 us
  Pallas kernels: 0 us -> 9.16 us
  other arithmetic: 7.91 us -> 0 us
  local copies, waits for them, and re-layouts: 7.13 us -> 0.69 us
  waiting for transfers between devices: 23.9 us -> 17.6 us
    all_to_all x0 -> x1, blocking collectives: none -> 18.1 us  [shards(): lax.all_to_all(strip, 'depth', split_axis=0, concat_axis=0, tiled=True)]
    ppermute x3 -> x0, starting transfers between devices: 14.1 us -> none  [swapped(): return lax.ppermute(block, axis, route)]
    pallas_call x0 -> x4, Pallas kernels: none -> 9.16 us  [the longest x1 3.6 us: blend(): pl.pallas_call(kernel, grid=(steps,), in_specs=[pl.BlockSpec((rows * 16,...]
    all_to_all x2 -> x1, starting transfers between devices: 25.9 us -> 19.1 us  [shards(): lax.all_to_all(blocks.reshape(owners, capacity * 4, width), ('tile', 'bri...]
    ppermute x3 -> x0, waiting for transfers between devices: 5.92 us -> none  [swapped(): return lax.ppermute(block, axis, route)]
    gather x4 -> x0, local copies, waits for them, and re-layouts: 3.24 us -> none  [the longest x2 2.02 us: shards(): screen = jnp.take(interlace, offsets[:, None] + along[None, :], axis=0)]
    mul x3 -> x0, other arithmetic: 3.12 us -> none  [the longest x1 2.54 us: order_layers(): chosen = chosen + picked[:, :, None, :] * layers[:, :, layer]]
    unnamed x13 -> x2, local copies, waits for them, and re-layouts: 2.76 us -> 0.69 us
  transfers between devices with their start and end apart: 5 -> 1, of which waited for: 5 -> 1; matrix products, arithmetic and copies ran while one was open for 5% -> 0% of each run, Pallas kernels for 0% -> 2%
where the time goes in v1:
time: 65.1 us; the launch traced here: 64.7 us
  starting transfers between devices  19.1 us (29%)
  blocking collectives  18.1 us (28%)
  waiting for transfers between devices  17.6 us (27%)
  Pallas kernels  9.16 us (14%)
  local copies, waits for them, and re-layouts  0.69 us (1%)
    all_to_all x1, starting transfers between devices, shards(): lax.all_to_all(blocks.reshape(owners, capacity * 4, width), ('tile', 'bri...  19.1 us
    all_to_all x1, blocking collectives, shards(): lax.all_to_all(strip, 'depth', split_axis=0, concat_axis=0, tiled=True)  18.1 us
    all_to_all x1, waiting for transfers between devices, shards(): lax.all_to_all(blocks.reshape(owners, capacity * 4, width), ('tile', 'bri...  17.6 us
    pallas_call x1, Pallas kernels, blend(): pl.pallas_call(kernel, grid=(steps,), in_specs=[pl.BlockSpec((rows * 16,...  3.6 us
    pallas_call x1, Pallas kernels, compose_strip(): pl.pallas_call(kernel, out_shape=jax.ShapeDtypeStruct((tiles, 4, slots //...  2.24 us
    pallas_call x1, Pallas kernels, stack(): pl.pallas_call(stack_kernel, out_shape=jax.ShapeDtypeStruct((share * 4, w...  1.71 us
    pallas_call x1, Pallas kernels, plan(): pl.pallas_call(plan_kernel, out_shape=(jax.ShapeDtypeStruct((total, total...  1.6 us
  transfers between devices with their start and end apart: 1, of which 1 were waited for; matrix products, arithmetic and copies ran while one was open for 0% of the time, Pallas kernels for 2%

profile of v1, /device:TPU:1, one launch (start us, length us, event | category | flops | bytes accessed | tf_op | source)
XLA Modules:
  0.0 64.7 jit_solution(17452352321331801900)
XLA Ops:
  0.0 3.6 %blend.1 = f32[512,128]{1,0:T(8,128)} custom-call(f32[2048,128]{1,0:T(8,128)} %bitcast.14, s32[512,128]{1,0:T(8,128)} %bitcast.16, s32[2,64]{1,0:T(2,128)} %bitcast.19), custom_call_target="tpu_custom_call" | custom-call | tf_op jit(solution)/shard_map/blend/pallas_call | solution.py:63
  3.6 19.1 %all-to-all-start = ((f32[64,8,128]{2,1,0:T(8,128)}), f32[64,8,128]{2,1,0:T(8,128)S(1)}, u32[]{:S(2)}, u32[]{:S(2)}) async-start(f32[64,8,128]{2,1,0:T(8,128)} %bitcast.15), calls=%async_computation | async-start | bytes 524288 | tf_op jit(solution)/shard_map/all_to_all | solution.py:180
  22.7 1.6 %plan.1 = (bf16[128,128]{1,0:T(8,128)(2,1)}, bf16[256,128]{1,0:T(8,128)(2,1)}) custom-call(s32[1,64]{1,0:T(1,128)} %bitcast.20, s32[2,64]{1,0:T(2,128)} %bitcast.17, s32[1,64]{1,0:T(1,128)} %order.1, s32[1,256]{1,0:T(1,128)} %bitcast.18), custom_call_target="tpu_custom_call" | custom-call | tf_op jit(solution)/shard_map/plan/pallas_call | solution.py:102
  24.3 17.6 %all-to-all-done = f32[64,8,128]{2,1,0:T(8,128)S(1)} async-done(((f32[64,8,128]{2,1,0:T(8,128)}), f32[64,8,128]{2,1,0:T(8,128)S(1)}, u32[]{:S(2)}, u32[]{:S(2)}) %all-to-all-start) | async-done | bytes 262176 | tf_op jit(solution)/shard_map/all_to_all | solution.py:180
  41.9 0.0 copy-start
  41.9 0.7 %copy-done = f32[64,8,128]{2,1,0:T(8,128)} copy-done((f32[64,8,128]{2,1,0:T(8,128)}, f32[64,8,128]{2,1,0:T(8,128)S(1)}, u32[]{:S(2)}) %copy-start) | copy-done | bytes 262168
  42.6 2.2 %strip.1 = f32[8,4,32,128]{3,2,1,0:T(8,128)} custom-call(f32[512,128]{1,0:T(8,128)} %bitcast.13, bf16[128,128]{1,0:T(8,128)(2,1)} %get-tuple-element.7.refs_1_, bf16[256,128]{1,0:T(8,128)(2,1)} %get-tuple-element.8.refs_2_), custom_call_target="tpu_custom_call" | custom-call | tf_op jit(solution)/shard_map/strip/pallas_call | solution.py:144
  44.9 18.1 %all_to_all.10.strips = f32[8,4,32,128]{3,2,1,0:T(8,128)} all-to-all(f32[8,4,32,128]{3,2,1,0:T(8,128)} %strip.1), channel_id=1, replica_groups=mesh['depth'=8,'tile'=16,'brick'=4] {'depth'}, dimensions={0} | all-to-all | bytes 1048576 | tf_op jit(solution)/shard_map/all_to_all | solution.py:185
  63.0 1.7 %stack.1 = f32[128,128]{1,0:T(8,128)} custom-call(f32[8,4,32,128]{3,2,1,0:T(8,128)} %all_to_all.10.strips), custom_call_target="tpu_custom_call" | custom-call | tf_op jit(solution)/shard_map/stack/pallas_call | solution.py:163
Async XLA Ops:
  3.6 38.3 %all-to-all-start = ((f32[64,8,128]{2,1,0:T(8,128)}), f32[64,8,128]{2,1,0:T(8,128)S(1)}, u32[]{:S(2)}, u32[]{:S(2)}) async-start(f32[64,8,128]{2,1,0:T(8,128)} %bitcast.15), calls=%async_computation | async-start | bytes 524288 | tf_op jit(solution)/shard_map/all_to_all | solution.py:180
  41.9 0.7 %copy-start = (f32[64,8,128]{2,1,0:T(8,128)}, f32[64,8,128]{2,1,0:T(8,128)S(1)}, u32[]{:S(2)}) copy-start(f32[64,8,128]{2,1,0:T(8,128)S(1)} %all-to-all-done) | copy-start | bytes 786436

commit v2 on v1

v2 whole, which is shorter than its diff:
```python
import jax
import jax.numpy as jnp
import numpy as np
from jax import lax
from jax.experimental import pallas as pl
from jax.experimental.pallas import tpu as pltpu
from jax.sharding import PartitionSpec as P


def resident(array):
    return pltpu.with_memory_space_constraint(array, pltpu.VMEM)


def columns(row, rows, width):
    length = row.shape[1]
    place = lax.broadcasted_iota(jnp.int32, (rows, length), 1)
    own = lax.broadcasted_iota(jnp.int32, (rows, length), 0)
    spread = jnp.where(place == own, row.astype(jnp.float32), 0.0).astype(jnp.bfloat16)
    return jnp.dot(spread, jnp.ones((length, width), jnp.bfloat16), preferred_element_type=jnp.float32)


def reorder(row, order):
    length = row.shape[1]
    source = lax.broadcasted_iota(jnp.int32, (length, length), 0)
    chosen = jnp.where(source == order, 1.0, 0.0).astype(jnp.bfloat16)
    rows = jnp.broadcast_to(row.astype(jnp.float32), (8, length)).astype(jnp.bfloat16)
    return jnp.dot(rows, chosen, preferred_element_type=jnp.float32)[0:1, :].astype(jnp.int32)


def halves(values):
    high = values.astype(jnp.bfloat16)
    low = (values - high.astype(jnp.float32)).astype(jnp.bfloat16)
    return high, low


def blend_kernel(order, steps, fragments, ranks, counts, out, pixels, layers, counted, mixed, *sems):
    owners = order.shape[0]
    capacity = counts.shape[0]
    width = out.shape[1]
    share = owners // steps

    def chunk(source, target, sem, rows, step):
        return pltpu.make_async_copy(source.at[pl.ds(step * rows, rows)], target.at[pl.ds(step * rows, rows)], sem.at[step])

    def copies(step):
        return (
            chunk(ranks, layers, sems[1], share * capacity * 4, step),
            chunk(fragments, pixels, sems[2], share * capacity * 16, step),
        )

    count_copy = pltpu.make_async_copy(counts, counted, sems[0])
    count_copy.start()
    for step in range(steps):
        for copy in copies(step):
            copy.start()
    count_copy.wait()
    pixel = lax.broadcasted_iota(jnp.int32, (owners, width), 1).astype(jnp.float32)
    visible = [
        jnp.where(pixel < columns(counted[slot : slot + 1, :], owners, width), 1.0, 0.0) for slot in range(capacity)
    ]
    for step in range(steps):
        for copy in copies(step):
            copy.wait()
        for slot in range(capacity):
            rank = [
                layers[pl.ds(step * share * capacity * 4 + slot * 4 + layer, share, stride=capacity * 4), :]
                for layer in range(4)
            ]
            entry = [
                [
                    pixels[
                        pl.ds(
                            step * share * capacity * 16 + slot * 16 + layer * 4 + part, share, stride=capacity * 16
                        ),
                        :,
                    ]
                    for part in range(4)
                ]
                for layer in range(4)
            ]
            clear = [1.0 - entry[layer][3] for layer in range(4)]
            weight = [visible[slot][step * share : (step + 1) * share]] * 4
            for one in range(4):
                for two in range(one + 1, 4):
                    ahead = rank[one] < rank[two]
                    weight[two] = weight[two] * jnp.where(ahead, clear[one], 1.0)
                    weight[one] = weight[one] * jnp.where(ahead, 1.0, clear[two])
            for part in range(4):
                total = entry[0][part] * weight[0]
                for layer in range(1, 4):
                    total = total + entry[layer][part] * weight[layer]
                mixed[pl.ds(step * share * capacity * 4 + slot * 4 + part, share, stride=capacity * 4), :] = total
    rows = capacity * 4
    for place, owner in enumerate(order):
        out[pl.ds(place * rows, rows), :] = mixed[pl.ds(int(owner) * rows, rows), :]


def blend(fragments, ranks, counts, order, steps):
    owners, capacity, _, width = fragments.shape
    rows = owners * capacity

    def kernel(*refs):
        blend_kernel(order, steps, *refs)

    return pl.pallas_call(
        kernel,
        in_specs=[pl.BlockSpec(memory_space=pl.ANY)] * 3,
        out_specs=pl.BlockSpec(memory_space=pltpu.VMEM),
        out_shape=pltpu.VMEM((rows * 4, width), jnp.float32),
        scratch_shapes=[
            pltpu.VMEM((rows * 16, width), jnp.float32),
            pltpu.VMEM((rows * 4, width), jnp.int32),
            pltpu.VMEM((capacity, owners), jnp.int32),
            pltpu.VMEM((rows * 4, width), jnp.float32),
            pltpu.SemaphoreType.DMA,
            pltpu.SemaphoreType.DMA((steps,)),
            pltpu.SemaphoreType.DMA((steps,)),
        ],
        name="blend",
    )(fragments.reshape(rows * 16, width), ranks.reshape(rows * 4, width), counts)


def plan_kernel(counts, runs, order, interlace, placed, earlier, target):
    capacity, bricks = runs.shape
    slots = interlace.shape[1]
    total = capacity * bricks
    place = placed[...]
    count = reorder(counts[...], place)
    rank = jnp.concatenate([reorder(order[...], place)] * capacity, axis=1)
    run = jnp.concatenate([reorder(runs[slot : slot + 1, :], place) for slot in range(capacity)], axis=1)
    live = jnp.concatenate([jnp.where(count > slot, 1, 0) for slot in range(capacity)], axis=1) > 0
    run_of = columns(run, total, total).astype(jnp.int32)
    rank_of = columns(rank, total, total).astype(jnp.int32)
    ahead = (run_of == run) & (rank < rank_of) & live
    earlier[...] = jnp.where(ahead, 1.0, 0.0).astype(jnp.bfloat16)
    slot_id = lax.broadcasted_iota(jnp.int32, (slots, total), 0)
    landing = jnp.where(slot_id == run, 1.0, 0.0).astype(jnp.bfloat16)
    screen = jnp.dot(
        jnp.broadcast_to(interlace[...].astype(jnp.float32), (8, slots)).astype(jnp.bfloat16),
        landing,
        preferred_element_type=jnp.float32,
    )[0:1, :].astype(jnp.int32)
    target[...] = jnp.where((slot_id == screen) & live, 1.0, 0.0).astype(jnp.bfloat16)


def plan(counts, runs, order, interlace, placed):
    capacity, bricks = runs.shape
    total = capacity * bricks
    slots = interlace.shape[1]
    return pl.pallas_call(
        plan_kernel,
        out_specs=(pl.BlockSpec(memory_space=pltpu.VMEM),) * 2,
        out_shape=(
            pltpu.VMEM((total, total), jnp.bfloat16),
            pltpu.VMEM((slots, total), jnp.bfloat16),
        ),
        name="plan",
    )(counts, runs, order, interlace, placed)


def strip_kernel(capacity, blocks, earlier, target, out):
    bricks = blocks.shape[0] // (capacity * 4)
    tiles, _, share, width = out.shape

    def part_of(part):
        return jnp.concatenate(
            [blocks[pl.ds(slot * 4 + part, bricks, stride=capacity * 4), :] for slot in range(capacity)],
            axis=0,
        )

    def picked(matrix, values):
        high, low = halves(values)
        return jnp.dot(matrix, high, preferred_element_type=jnp.float32) + jnp.dot(
            matrix, low, preferred_element_type=jnp.float32
        )

    alpha = part_of(3)
    passed = jnp.exp(picked(earlier[...], jnp.log(1.0 - alpha)))
    shaded = jnp.concatenate([part_of(0) * passed, part_of(1) * passed, part_of(2) * passed, alpha * passed], axis=1)
    strip = picked(target[...], shaded)
    for tile in range(tiles):
        for part in range(4):
            out[tile, part] = strip[tile * share : (tile + 1) * share, part * width : (part + 1) * width]


def compose_strip(blocks, earlier, target, capacity, tiles):
    width = blocks.shape[1]
    slots = target.shape[0]

    def kernel(*refs):
        strip_kernel(capacity, *refs)

    return pl.pallas_call(
        kernel,
        in_specs=[pl.BlockSpec(memory_space=pltpu.VMEM)] * 3,
        out_specs=pl.BlockSpec(memory_space=pltpu.VMEM),
        out_shape=pltpu.VMEM((tiles, 4, slots // tiles, width), jnp.float32),
        name="strip",
    )(resident(blocks), resident(earlier), resident(target))


def stack_kernel(strips, out):
    slabs, _, share, _ = strips.shape
    total = [strips[slabs - 1, part] for part in range(4)]
    for slab in range(slabs - 2, -1, -1):
        clear = 1.0 - strips[slab, 3]
        total = [strips[slab, part] + clear * total[part] for part in range(4)]
    for part in range(4):
        out[pl.ds(part, share, stride=4), :] = total[part]


def stack(strips):
    _, _, share, width = strips.shape
    return pl.pallas_call(
        stack_kernel,
        in_specs=[pl.BlockSpec(memory_space=pltpu.VMEM)],
        out_shape=jax.ShapeDtypeStruct((share * 4, width), jnp.float32),
        name="stack",
    )(resident(strips))


def exchange_order(tiles, bricks):
    return np.array(
        [
            (tile + tiles // 2 + 1) % tiles * bricks + (brick + tile + bricks // 2) % bricks
            for brick in range(bricks)
            for tile in range(tiles)
        ],
        np.int32,
    )


def shards(fragments, layer_rank, pixel_count, slot_count, block_run, brick_order, interlace):
    _, _, owners, capacity, _, width = fragments.shape
    slots = interlace.shape[0]
    tiles = lax.axis_size("depth")
    order = exchange_order(lax.axis_size("tile"), lax.axis_size("brick"))
    blocks = blend(fragments[0, 0], layer_rank[0, 0], pixel_count[0, 0].T, order, 4)
    sent = lax.all_to_all(
        blocks.reshape(owners, capacity * 4, width),
        ("tile", "brick"),
        split_axis=0,
        concat_axis=0,
        tiled=True,
        axis_index_groups=[order.tolist()],
    )
    earlier, target = plan(
        slot_count[0], block_run[0, 0].T, brick_order, interlace.reshape(1, slots), jnp.asarray(order).reshape(1, owners)
    )
    strip = compose_strip(sent.reshape(owners * capacity * 4, width), earlier, target, capacity, tiles)
    strips = lax.all_to_all(strip, "depth", split_axis=0, concat_axis=0, tiled=True)
    return stack(strips).reshape(1, 1, slots // tiles, 4, width)


def solution(mesh):
    return jax.shard_map(
        shards,
        mesh=mesh,
        in_specs=(
            P("depth", ("tile", "brick"), None, None, None, None),
            P("depth", ("tile", "brick"), None, None, None),
            P("depth", ("tile", "brick"), None, None),
            P("depth", ("tile", "brick"), None),
            P("depth", ("tile", "brick"), None, None),
            P("depth", None),
            P(),
        ),
        out_specs=P(("tile", "brick"), "depth", None, None, None),
        check_vma=False,
    )
```

time: 65.1 us -> 53 us (0.81)
  waiting for transfers between devices: 17.6 us -> 11.2 us
  Pallas kernels: 9.16 us -> 4.83 us
  blocking collectives: 18.1 us -> 14.6 us
  starting transfers between devices: 19.1 us -> 22.1 us
  local copies, waits for them, and re-layouts: 0.69 us -> 0 us
    all_to_all x1, waiting for transfers between devices: 17.6 us -> 11.2 us  [shards(): lax.all_to_all(blocks.reshape(owners, capacity * 4, width), ('tile', 'bri...]
    pallas_call x4, Pallas kernels: 9.16 us -> 4.83 us  [the longest x1 2.59 us: blend(): pl.pallas_call(kernel, in_specs=[pl.BlockSpec(memory_space=pl.ANY)] * 3,...]
    all_to_all x1, blocking collectives: 18.1 us -> 14.6 us  [shards(): lax.all_to_all(strip, 'depth', split_axis=0, concat_axis=0, tiled=True)]
    all_to_all x1, starting transfers between devices: 19.1 us -> 22.1 us  [shards(): lax.all_to_all(blocks.reshape(owners, capacity * 4, width), ('tile', 'bri...]
    unnamed x2 -> x0, local copies, waits for them, and re-layouts: 0.69 us -> none
where the time goes in v2:
time: 53 us; the launch traced here: 52.8 us
  starting transfers between devices  22.1 us (42%)
  blocking collectives  14.6 us (28%)
  waiting for transfers between devices  11.2 us (21%)
  Pallas kernels  4.83 us (9%)
    all_to_all x1, starting transfers between devices, shards(): lax.all_to_all(blocks.reshape(owners, capacity * 4, width), ('tile', 'bri...  22.1 us
    all_to_all x1, blocking collectives, shards(): lax.all_to_all(strip, 'depth', split_axis=0, concat_axis=0, tiled=True)  14.6 us
    all_to_all x1, waiting for transfers between devices, shards(): lax.all_to_all(blocks.reshape(owners, capacity * 4, width), ('tile', 'bri...  11.2 us
    pallas_call x1, Pallas kernels, blend(): pl.pallas_call(kernel, in_specs=[pl.BlockSpec(memory_space=pl.ANY)] * 3,...  2.59 us
    pallas_call x1, Pallas kernels, plan(): pl.pallas_call(plan_kernel, out_specs=(pl.BlockSpec(memory_space=pltpu.VM...  1.1 us
  transfers between devices with their start and end apart: 1, of which 1 were waited for; matrix products, arithmetic and copies ran while one was open for 0% of the time, Pallas kernels for 2%

profile of v2, /device:TPU:1, one launch (start us, length us, event | category | flops | bytes accessed | tf_op | source)
XLA Modules:
  0.0 52.8 jit_solution(5897950395641897447)
XLA Ops:
  0.0 2.6 %blend.1 = f32[512,128]{1,0:T(8,128)} custom-call(f32[2048,128]{1,0:T(8,128)} %bitcast.14, s32[512,128]{1,0:T(8,128)} %bitcast.15, s32[2,64]{1,0:T(2,128)} %bitcast.18), custom_call_target="tpu_custom_call" | custom-call | tf_op jit(solution)/shard_map/blend/pallas_call | solution.py:105
  2.6 22.1 %all-to-all-start = ((f32[64,8,128]{2,1,0:T(8,128)}), f32[64,8,128]{2,1,0:T(8,128)S(1)}, u32[]{:S(2)}, u32[]{:S(2)}) async-start(f32[64,8,128]{2,1,0:T(8,128)} %bitcast.4), calls=%async_computation | async-start | bytes 524288 | tf_op jit(solution)/shard_map/all_to_all | solution.py:239
  24.7 1.1 %plan.1 = (bf16[128,128]{1,0:T(8,128)(2,1)S(1)}, bf16[256,128]{1,0:T(8,128)(2,1)S(1)}) custom-call(s32[1,64]{1,0:T(1,128)} %bitcast.19, s32[2,64]{1,0:T(2,128)} %bitcast.16, s32[1,64]{1,0:T(1,128)} %order.1, s32[1,256]{1,0:T(1,128)} %bitcast.17, s32[1,64]{1,0:T(1,128)} %constant.9.placed), custom_call_target="tpu_custom_call" | custom-call | tf_op jit(solution)/shard_map/plan/pallas_call | solution.py:150
  25.8 11.2 %all-to-all-done = f32[64,8,128]{2,1,0:T(8,128)S(1)} async-done(((f32[64,8,128]{2,1,0:T(8,128)}), f32[64,8,128]{2,1,0:T(8,128)S(1)}, u32[]{:S(2)}, u32[]{:S(2)}) %all-to-all-start) | async-done | bytes 262176 | tf_op jit(solution)/shard_map/all_to_all | solution.py:239
  37.0 0.5 strip.1
  37.5 14.6 %all_to_all.10.strips = f32[8,4,32,128]{3,2,1,0:T(8,128)S(1)} all-to-all(f32[8,4,32,128]{3,2,1,0:T(8,128)S(1)} %strip.1), channel_id=1, replica_groups=mesh['depth'=8,'tile'=16,'brick'=4] {'depth'}, dimensions={0} | all-to-all | bytes 1048576 | tf_op jit(solution)/shard_map/all_to_all | solution.py:251
  52.1 0.7 %stack.1 = f32[128,128]{1,0:T(8,128)} custom-call(f32[8,4,32,128]{3,2,1,0:T(8,128)S(1)} %all_to_all.10.strips), custom_call_target="tpu_custom_call" | custom-call | tf_op jit(solution)/shard_map/stack/pallas_call | solution.py:214
Async XLA Ops:
  2.6 34.4 %all-to-all-start = ((f32[64,8,128]{2,1,0:T(8,128)}), f32[64,8,128]{2,1,0:T(8,128)S(1)}, u32[]{:S(2)}, u32[]{:S(2)}) async-start(f32[64,8,128]{2,1,0:T(8,128)} %bitcast.4), calls=%async_computation | async-start | bytes 524288 | tf_op jit(solution)/shard_map/all_to_all | solution.py:239

commit v3 on v2

v3 whole, which is shorter than its diff:
```python
import jax
import jax.numpy as jnp
import numpy as np
from jax import lax
from jax.experimental import pallas as pl
from jax.experimental.pallas import tpu as pltpu
from jax.sharding import PartitionSpec as P


def resident(array):
    return pltpu.with_memory_space_constraint(array, pltpu.VMEM)


def columns(row, rows, width):
    length = row.shape[1]
    place = lax.broadcasted_iota(jnp.int32, (rows, length), 1)
    own = lax.broadcasted_iota(jnp.int32, (rows, length), 0)
    spread = jnp.where(place == own, row.astype(jnp.float32), 0.0).astype(jnp.bfloat16)
    return jnp.dot(spread, jnp.ones((length, width), jnp.bfloat16), preferred_element_type=jnp.float32)


def reorder(row, order):
    length = row.shape[1]
    source = lax.broadcasted_iota(jnp.int32, (length, length), 0)
    chosen = jnp.where(source == order, 1.0, 0.0).astype(jnp.bfloat16)
    rows = jnp.broadcast_to(row.astype(jnp.float32), (8, length)).astype(jnp.bfloat16)
    return jnp.dot(rows, chosen, preferred_element_type=jnp.float32)[0:1, :].astype(jnp.int32)


def halves(values):
    high = values.astype(jnp.bfloat16)
    low = (values - high.astype(jnp.float32)).astype(jnp.bfloat16)
    return high, low


def picked(matrix, values):
    high, low = halves(values)
    return jnp.dot(matrix, high, preferred_element_type=jnp.float32) + jnp.dot(
        matrix, low, preferred_element_type=jnp.float32
    )


def turned(values):
    return pltpu.roll(values, values.shape[-1] // 2, values.ndim - 1)


def in_left(values):
    lane = lax.broadcasted_iota(jnp.int32, values.shape, values.ndim - 1)
    return lane < values.shape[-1] // 2


def lefts(one, two):
    return jnp.where(in_left(one), one, turned(two))


def rights(one, two):
    return jnp.where(in_left(one), turned(one), two)


def blend_kernel(root, steps, fragments, ranks, counts, out, pixels, layers, counted, *sems):
    capacity, owners = counts.shape
    width = out.shape[1]
    share = owners // steps

    def chunk(source, target, sem, rows, step):
        return pltpu.make_async_copy(source.at[pl.ds(step * rows, rows)], target.at[pl.ds(step * rows, rows)], sem.at[step])

    def copies(step):
        return (
            chunk(ranks, layers, sems[1], share * capacity * 4, step),
            chunk(fragments, pixels, sems[2], share * capacity * 16, step),
        )

    count_copy = pltpu.make_async_copy(counts, counted, sems[0])
    count_copy.start()
    for step in range(steps):
        for copy in copies(step):
            copy.start()
    count_copy.wait()
    pixel = lax.broadcasted_iota(jnp.int32, (owners, width), 1).astype(jnp.float32)
    visible = [
        jnp.where(pixel < columns(counted[slot : slot + 1, :], owners, width), 1.0, 0.0) for slot in range(capacity)
    ]
    for step in range(steps):
        for copy in copies(step):
            copy.wait()
        blended = []
        for slot in range(capacity):
            rank = [
                layers[pl.ds(step * share * capacity * 4 + slot * 4 + layer, share, stride=capacity * 4), :]
                for layer in range(4)
            ]
            entry = [
                [
                    pixels[
                        pl.ds(
                            step * share * capacity * 16 + slot * 16 + layer * 4 + part, share, stride=capacity * 16
                        ),
                        :,
                    ]
                    for part in range(4)
                ]
                for layer in range(4)
            ]
            clear = [1.0 - entry[layer][3] for layer in range(4)]
            weight = [visible[slot][step * share : (step + 1) * share]] * 4
            for one in range(4):
                for two in range(one + 1, 4):
                    ahead = rank[one] < rank[two]
                    weight[two] = weight[two] * jnp.where(ahead, clear[one], 1.0)
                    weight[one] = weight[one] * jnp.where(ahead, 1.0, clear[two])
            mixed = []
            for part in range(4):
                total = entry[0][part] * weight[0]
                for layer in range(1, 4):
                    total = total + entry[layer][part] * weight[layer]
                mixed.append(total)
            blended.append(mixed)
        for part in range(4):
            one, two = blended[0][part], blended[1][part]
            out[pl.ds(step * share * 4 + part, share, stride=4), :] = rights(one, two)
            out[pl.ds((owners + step * share) * 4 + part, share, stride=4), :] = lefts(one, two)
    for half in range(2):
        first = pl.ds(half * owners * 4, 4)
        other = pl.ds((half * owners + root) * 4, 4)
        moved = out[first, :]
        out[first, :] = out[other, :]
        out[other, :] = moved


def blend(fragments, ranks, counts, root, steps):
    owners, capacity, _, width = fragments.shape
    rows = owners * capacity

    def kernel(*refs):
        blend_kernel(root, steps, *refs)

    return pl.pallas_call(
        kernel,
        in_specs=[pl.BlockSpec(memory_space=pl.ANY)] * 3,
        out_specs=pl.BlockSpec(memory_space=pltpu.VMEM),
        out_shape=jax.ShapeDtypeStruct((rows * 4, width), jnp.float32),
        scratch_shapes=[
            pltpu.VMEM((rows * 16, width), jnp.float32),
            pltpu.VMEM((rows * 4, width), jnp.int32),
            pltpu.VMEM((capacity, owners), jnp.int32),
            pltpu.SemaphoreType.DMA,
            pltpu.SemaphoreType.DMA((steps,)),
            pltpu.SemaphoreType.DMA((steps,)),
        ],
        name="blend",
    )(fragments.reshape(rows * 16, width), ranks.reshape(rows * 4, width), counts)


def plan_kernel(capacity, index, interlace, placed, earlier, target):
    bricks = placed.shape[1]
    slots = interlace.shape[1]
    total = capacity * bricks
    place = placed[...]
    for slab in range(2):
        count = reorder(index[slab, 0:1, :], place)
        rank = jnp.concatenate([reorder(index[slab, 1:2, :], place)] * capacity, axis=1)
        run = jnp.concatenate(
            [reorder(index[slab, 2 + slot : 3 + slot, :], place) for slot in range(capacity)], axis=1
        )
        live = jnp.concatenate([jnp.where(count > slot, 1, 0) for slot in range(capacity)], axis=1) > 0
        run_of = columns(run, total, total).astype(jnp.int32)
        rank_of = columns(rank, total, total).astype(jnp.int32)
        ahead = (run_of == run) & (rank < rank_of) & live
        earlier[:, slab * total : (slab + 1) * total] = jnp.where(ahead, 1.0, 0.0).astype(jnp.bfloat16)
        slot_id = lax.broadcasted_iota(jnp.int32, (slots, total), 0)
        landing = jnp.where(slot_id == run, 1.0, 0.0).astype(jnp.bfloat16)
        screen = jnp.dot(
            jnp.broadcast_to(interlace[...].astype(jnp.float32), (8, slots)).astype(jnp.bfloat16),
            landing,
            preferred_element_type=jnp.float32,
        )[0:1, :].astype(jnp.int32)
        target[:, slab * total : (slab + 1) * total] = jnp.where((slot_id == screen) & live, 1.0, 0.0).astype(
            jnp.bfloat16
        )


def plan(index, interlace, placed, capacity):
    total = capacity * placed.shape[1]
    slots = interlace.shape[1]

    def kernel(*refs):
        plan_kernel(capacity, *refs)

    return pl.pallas_call(
        kernel,
        out_specs=(pl.BlockSpec(memory_space=pltpu.VMEM),) * 2,
        out_shape=(
            pltpu.VMEM((total, 2 * total), jnp.bfloat16),
            pltpu.VMEM((slots, 2 * total), jnp.bfloat16),
        ),
        name="plan",
    )(index, interlace, placed)


def strip_kernel(blocks, earlier, target, out):
    bricks = blocks.shape[0] // 8
    tiles, _, share, width = out.shape

    def part_of(part):
        back = blocks[pl.ds(part, bricks, stride=4), :]
        front = blocks[pl.ds(bricks * 4 + part, bricks, stride=4), :]
        return jnp.concatenate([lefts(front, back), rights(front, back)], axis=0)

    def apart(values):
        left = in_left(values)
        return jnp.concatenate([jnp.where(left, values, 0.0), jnp.where(left, 0.0, values)], axis=0)

    parts = [part_of(part) for part in range(4)]
    passed = jnp.exp(picked(earlier[...], apart(jnp.log(1.0 - parts[3]))))
    shaded = jnp.concatenate([apart(part * passed) for part in parts], axis=1)
    strip = picked(target[...], shaded)
    strips = [strip[:, part * width : (part + 1) * width] for part in range(4)]
    clear = 1.0 - lefts(strips[3], strips[3])
    for pair in range(2):
        one, two = strips[2 * pair], strips[2 * pair + 1]
        merged = lefts(one, two) + clear * rights(one, two)
        for tile in range(tiles):
            out[tile, pair] = merged[tile * share : (tile + 1) * share]


def compose_strip(blocks, earlier, target, tiles):
    width = blocks.shape[1]
    slots = target.shape[0]
    return pl.pallas_call(
        strip_kernel,
        in_specs=[pl.BlockSpec(memory_space=pltpu.VMEM)] * 3,
        out_specs=pl.BlockSpec(memory_space=pltpu.VMEM),
        out_shape=pltpu.VMEM((tiles, 2, slots // tiles, width), jnp.float32),
        name="strip",
    )(resident(blocks), resident(earlier), resident(target))


def stack_kernel(strips, out):
    slabs, _, share, _ = strips.shape
    totals = []
    for half in range(2):
        total = [strips[slabs - 2 + half, pair] for pair in range(2)]
        for slab in range(slabs - 4, -1, -2):
            front = [strips[slab + half, pair] for pair in range(2)]
            clear = 1.0 - jnp.where(in_left(front[1]), turned(front[1]), front[1])
            total = [front[pair] + clear * total[pair] for pair in range(2)]
        totals.append(total)
    for pair in range(2):
        out[pl.ds(2 * pair, share, stride=4), :] = lefts(totals[0][pair], totals[1][pair])
        out[pl.ds(2 * pair + 1, share, stride=4), :] = rights(totals[0][pair], totals[1][pair])


def stack(strips):
    _, _, share, width = strips.shape
    return pl.pallas_call(
        stack_kernel,
        in_specs=[pl.BlockSpec(memory_space=pltpu.VMEM)],
        out_shape=jax.ShapeDtypeStruct((share * 4, width), jnp.float32),
        name="stack",
    )(resident(strips))


def shards(fragments, layer_rank, pixel_count, slot_count, block_run, brick_order, interlace):
    _, _, owners, capacity, _, width = fragments.shape
    slots = interlace.shape[0]
    tiles = lax.axis_size("depth")
    bricks = lax.axis_size("brick")
    root = (lax.axis_size("tile") // 2 + 1) * bricks + bricks // 2
    order = np.arange(owners, dtype=np.int32)
    order[0], order[root] = root, 0
    blocks = blend(fragments[0, 0], layer_rank[0, 0], pixel_count[0, 0].T, root, 4)
    groups = [
        [int(owners * (2 * chip + core) + owner) for core in (1, 0) for owner in order] for chip in range(tiles // 2)
    ]
    sent = lax.all_to_all(
        blocks.reshape(2 * owners, 4, width),
        ("depth", "tile", "brick"),
        split_axis=0,
        concat_axis=0,
        tiled=True,
        axis_index_groups=groups,
    )
    own = jnp.concatenate([slot_count[0], brick_order, block_run[0, 0].T], axis=0)
    other = lax.ppermute(own, "depth", [(place, place ^ 1) for place in range(tiles)])
    in_front = lax.axis_index("depth") % 2 == 0
    index = jnp.stack([jnp.where(in_front, own, other), jnp.where(in_front, other, own)])
    earlier, target = plan(index, interlace.reshape(1, slots), jnp.asarray(order).reshape(1, owners), capacity)
    strip = compose_strip(sent.reshape(owners * 8, width), earlier, target, tiles)
    strips = lax.all_to_all(strip, "depth", split_axis=0, concat_axis=0, tiled=True)
    return stack(strips).reshape(1, 1, slots // tiles, 4, width)


def solution(mesh):
    return jax.shard_map(
        shards,
        mesh=mesh,
        in_specs=(
            P("depth", ("tile", "brick"), None, None, None, None),
            P("depth", ("tile", "brick"), None, None, None),
            P("depth", ("tile", "brick"), None, None),
            P("depth", ("tile", "brick"), None),
            P("depth", ("tile", "brick"), None, None),
            P("depth", None),
            P(),
        ),
        out_specs=P(("tile", "brick"), "depth", None, None, None),
        check_vma=False,
    )
```

time: 53 us -> 51.9 us (0.979)
  starting transfers between devices: 22.1 us -> 26.1 us
  waiting for transfers between devices: 11.2 us -> 7.3 us
  blocking collectives: 14.6 us -> 11.2 us
  Pallas kernels: 4.83 us -> 5.71 us
  local copies, waits for them, and re-layouts: 0 us -> 0.66 us
  other arithmetic: 0 us -> 0.62 us
    all_to_all x1, waiting for transfers between devices: 11.2 us -> 6.51 us  [shards(): lax.all_to_all(blocks.reshape(2 * owners, 4, width), ('depth', 'tile', 'b...]
    all_to_all x1, blocking collectives: 14.6 us -> 11.2 us  [shards(): lax.all_to_all(strip, 'depth', split_axis=0, concat_axis=0, tiled=True)]
    ppermute x0 -> x1, starting transfers between devices: none -> 2.74 us  [shards(): lax.ppermute(own, 'depth', [(place, place ^ 1) for place in range(tiles)])]
    all_to_all x1, starting transfers between devices: 22.1 us -> 23.4 us  [shards(): lax.all_to_all(blocks.reshape(2 * owners, 4, width), ('depth', 'tile', 'b...]
    ppermute x0 -> x1, waiting for transfers between devices: none -> 0.79 us  [shards(): lax.ppermute(own, 'depth', [(place, place ^ 1) for place in range(tiles)])]
    unnamed x0 -> x6, local copies, waits for them, and re-layouts: none -> 0.66 us
    another operation x0 -> x2, other arithmetic: none -> 0.61 us  [shards(): jnp.stack([jnp.where(in_front, own, other), jnp.where(in_front, other, ow...]
  transfers between devices with their start and end apart: 1 -> 2, of which waited for: 1 -> 2; matrix products, arithmetic and copies ran while one was open for 0% -> 1% of each run, Pallas kernels for 2% -> 3%
where the time goes in v3:
time: 51.9 us; the launch traced here: 51.6 us
  starting transfers between devices  26.1 us (50%)
  blocking collectives  11.2 us (22%)
  waiting for transfers between devices  7.3 us (14%)
  Pallas kernels  5.71 us (11%)
  local copies, waits for them, and re-layouts  0.66 us (1%)
  other arithmetic  0.62 us (1%)
    all_to_all x1, starting transfers between devices, shards(): lax.all_to_all(blocks.reshape(2 * owners, 4, width), ('depth', 'tile', 'b...  23.4 us
    all_to_all x1, blocking collectives, shards(): lax.all_to_all(strip, 'depth', split_axis=0, concat_axis=0, tiled=True)  11.2 us
    all_to_all x1, waiting for transfers between devices, shards(): lax.all_to_all(blocks.reshape(2 * owners, 4, width), ('depth', 'tile', 'b...  6.51 us
    pallas_call x1, Pallas kernels, blend(): pl.pallas_call(kernel, in_specs=[pl.BlockSpec(memory_space=pl.ANY)] * 3,...  2.84 us
    ppermute x1, starting transfers between devices, shards(): lax.ppermute(own, 'depth', [(place, place ^ 1) for place in range(tiles)])  2.74 us
    pallas_call x1, Pallas kernels, plan(): pl.pallas_call(kernel, out_specs=(pl.BlockSpec(memory_space=pltpu.VMEM),)...  1.32 us
  transfers between devices with their start and end apart: 2, of which 2 were waited for; matrix products, arithmetic and copies ran while one was open for 1% of the time, Pallas kernels for 3%

profile of v3, /device:TPU:1, one launch (start us, length us, event | category | flops | bytes accessed | tf_op | source)
XLA Modules:
  0.0 51.6 jit_solution(3709816733477304947)
XLA Ops:
  0.0 2.8 %blend.1 = f32[512,128]{1,0:T(8,128)} custom-call(f32[2048,128]{1,0:T(8,128)} %bitcast.18, s32[512,128]{1,0:T(8,128)} %bitcast.20, s32[2,64]{1,0:T(2,128)} %bitcast.26), custom_call_target="tpu_custom_call" | custom-call | tf_op jit(solution)/shard_map/blend/pallas_call | solution.py:138
  2.9 0.0 copy-start.2
  2.9 23.4 %all-to-all-start = ((f32[128,4,128]{2,1,0:T(4,128)}), f32[128,4,128]{2,1,0:T(4,128)S(1)}, u32[]{:S(2)}, u32[]{:S(2)}) async-start(f32[128,4,128]{2,1,0:T(4,128)} %bitcast.19), calls=%async_computation | async-start | bytes 524288 | tf_op jit(solution)/shard_map/all_to_all | solution.py:276
  26.2 0.0 copy-start
  26.2 0.0 copy-start.1
  26.2 0.0 copy-done.2
  26.3 0.6 %copy-done = s32[1,1,64,2]{2,3,1,0:T(2,128)S(1)} copy-done((s32[1,1,64,2]{2,3,1,0:T(2,128)S(1)}, s32[1,1,64,2]{2,3,1,0:T(2,128)}, u32[]{:S(2)}) %copy-start) | copy-done | bytes 536
  26.9 0.0 copy-done.1
  26.9 2.7 %collective-permute-start = (s32[4,64]{1,0:T(4,128)S(1)}, s32[4,64]{1,0:T(4,128)S(1)}, u32[]{:S(2)}, u32[]{:S(2)}) collective-permute-start(s32[4,64]{1,0:T(4,128)S(1)} %pad_add_fusion.1), channel_id=1, source_target_pairs={{0,64},{64,0},{128,192},{192,128},{256,320},{320,256},{384,448},{4... | collective-permute-start | bytes 3080 | tf_op jit(solution)/shard_map/ppermute | solution.py:285
  29.7 0.8 %collective-permute-done = s32[4,64]{1,0:T(4,128)S(1)} collective-permute-done((s32[4,64]{1,0:T(4,128)S(1)}, s32[4,64]{1,0:T(4,128)S(1)}, u32[]{:S(2)}, u32[]{:S(2)}) %collective-permute-start) | collective-permute-done | bytes 1056 | tf_op jit(solution)/shard_map/ppermute | solution.py:285
  30.5 0.6 %pad_add_fusion.refs_0_ = s32[2,4,64]{2,1,0:T(4,128)} fusion(s32[1,4,64]{2,1,0:T(4,128)S(1)} %get-tuple-element.10, s32[1,4,64]{2,1,0:T(4,128)S(1)} %get-tuple-element.9), kind=kLoop, calls=%fused_computation | loop fusion | flops 512 | bytes 4096 | tf_op jit(solution)/shard_map/stack | solution.py:287
  31.1 1.3 %plan.1 = (bf16[128,256]{1,0:T(8,128)(2,1)S(1)}, bf16[256,256]{1,0:T(8,128)(2,1)S(1)}) custom-call(s32[2,4,64]{2,1,0:T(4,128)} %pad_add_fusion.refs_0_, s32[1,256]{1,0:T(1,128)} %bitcast.25, s32[1,64]{1,0:T(1,128)} %constant.29.refs_2_), custom_call_target="tpu_custom_call" | custom-call | tf_op jit(solution)/shard_map/plan/pallas_call | solution.py:190
  32.4 6.5 %all-to-all-done = f32[128,4,128]{2,1,0:T(4,128)S(1)} async-done(((f32[128,4,128]{2,1,0:T(4,128)}), f32[128,4,128]{2,1,0:T(4,128)S(1)}, u32[]{:S(2)}, u32[]{:S(2)}) %all-to-all-start) | async-done | bytes 262176 | tf_op jit(solution)/shard_map/all_to_all | solution.py:276
  38.9 0.7 %strip.1 = f32[8,2,32,128]{3,2,1,0:T(8,128)S(1)} custom-call(f32[512,128]{1,0:T(8,128)S(1)} %bitcast.17, bf16[128,256]{1,0:T(8,128)(2,1)S(1)} %get-tuple-element.7.earlier, bf16[256,256]{1,0:T(8,128)(2,1)S(1)} %get-tuple-element.8.target), custom_call_target="tpu_custom_call" | custom-call | tf_op jit(solution)/shard_map/strip/pallas_call | solution.py:230
  39.7 11.2 %all_to_all.10.strips = f32[8,2,32,128]{3,2,1,0:T(8,128)S(1)} all-to-all(f32[8,2,32,128]{3,2,1,0:T(8,128)S(1)} %strip.1), channel_id=1, replica_groups=mesh['depth'=8,'tile'=16,'brick'=4] {'depth'}, dimensions={0} | all-to-all | bytes 524288 | tf_op jit(solution)/shard_map/all_to_all | solution.py:290
  50.8 0.8 %stack.13 = f32[128,128]{1,0:T(8,128)} custom-call(f32[8,2,32,128]{3,2,1,0:T(8,128)S(1)} %all_to_all.10.strips), custom_call_target="tpu_custom_call" | custom-call | tf_op jit(solution)/shard_map/stack/pallas_call | solution.py:256
  (2 shorter events, 0.0 us)
Async XLA Ops:
  2.9 23.4 %copy-start.2 = (s32[1,1,64]{2,1,0:T(1,128)S(1)}, s32[1,1,64]{2,1,0:T(1,128)}, u32[]{:S(2)}) copy-start(s32[1,1,64]{2,1,0:T(1,128)} %param.11) | copy-start | bytes 772
  2.9 36.1 %all-to-all-start = ((f32[128,4,128]{2,1,0:T(4,128)}), f32[128,4,128]{2,1,0:T(4,128)S(1)}, u32[]{:S(2)}, u32[]{:S(2)}) async-start(f32[128,4,128]{2,1,0:T(4,128)} %bitcast.19), calls=%async_computation | async-start | bytes 524288 | tf_op jit(solution)/shard_map/all_to_all | solution.py:276
  26.2 0.7 %copy-start = (s32[1,1,64,2]{2,3,1,0:T(2,128)S(1)}, s32[1,1,64,2]{2,3,1,0:T(2,128)}, u32[]{:S(2)}) copy-start(s32[1,1,64,2]{2,3,1,0:T(2,128)} %param.12) | copy-start | bytes 1540
  26.2 0.7 %copy-start.1 = (s32[1,64]{1,0:T(1,128)S(1)}, s32[1,64]{1,0:T(1,128)}, u32[]{:S(2)}) copy-start(s32[1,64]{1,0:T(1,128)} %param.13) | copy-start | bytes 772
  26.9 3.5 %collective-permute-start = (s32[4,64]{1,0:T(4,128)S(1)}, s32[4,64]{1,0:T(4,128)S(1)}, u32[]{:S(2)}, u32[]{:S(2)}) collective-permute-start(s32[4,64]{1,0:T(4,128)S(1)} %pad_add_fusion.1), channel_id=1, source_target_pairs={{0,64},{64,0},{128,192},{192,128},{256,320},{320,256},{384,448},{4... | collective-permute-start | bytes 3080 | tf_op jit(solution)/shard_map/ppermute | solution.py:285

commit v4 on v3

--- a/solution.py
+++ b/solution.py
@@ -198,7 +198,7 @@
     )(index, interlace, placed)
 
 
-def strip_kernel(blocks, earlier, target, out):
+def strip_kernel(first, blocks, earlier, target, out):
     bricks = blocks.shape[0] // 8
     tiles, _, share, width = out.shape
 
@@ -221,14 +221,18 @@
         one, two = strips[2 * pair], strips[2 * pair + 1]
         merged = lefts(one, two) + clear * rights(one, two)
         for tile in range(tiles):
-            out[tile, pair] = merged[tile * share : (tile + 1) * share]
-
-
-def compose_strip(blocks, earlier, target, tiles):
+            out[tile ^ first, pair] = merged[tile * share : (tile + 1) * share]
+
+
+def compose_strip(blocks, earlier, target, tiles, first):
     width = blocks.shape[1]
     slots = target.shape[0]
+
+    def kernel(*refs):
+        strip_kernel(first, *refs)
+
     return pl.pallas_call(
-        strip_kernel,
+        kernel,
         in_specs=[pl.BlockSpec(memory_space=pltpu.VMEM)] * 3,
         out_specs=pl.BlockSpec(memory_space=pltpu.VMEM),
         out_shape=pltpu.VMEM((tiles, 2, slots // tiles, width), jnp.float32),
@@ -236,13 +240,13 @@
     )(resident(blocks), resident(earlier), resident(target))
 
 
-def stack_kernel(strips, out):
+def stack_kernel(first, strips, out):
     slabs, _, share, _ = strips.shape
     totals = []
     for half in range(2):
-        total = [strips[slabs - 2 + half, pair] for pair in range(2)]
+        total = [strips[(slabs - 2 + half) ^ first, pair] for pair in range(2)]
         for slab in range(slabs - 4, -1, -2):
-            front = [strips[slab + half, pair] for pair in range(2)]
+            front = [strips[(slab + half) ^ first, pair] for pair in range(2)]
             clear = 1.0 - jnp.where(in_left(front[1]), turned(front[1]), front[1])
             total = [front[pair] + clear * total[pair] for pair in range(2)]
         totals.append(total)
@@ -251,10 +255,14 @@
         out[pl.ds(2 * pair + 1, share, stride=4), :] = rights(totals[0][pair], totals[1][pair])
 
 
-def stack(strips):
+def stack(strips, first):
     _, _, share, width = strips.shape
+
+    def kernel(*refs):
+        stack_kernel(first, *refs)
+
     return pl.pallas_call(
-        stack_kernel,
+        kernel,
         in_specs=[pl.BlockSpec(memory_space=pltpu.VMEM)],
         out_shape=jax.ShapeDtypeStruct((share * 4, width), jnp.float32),
         name="stack",
@@ -266,6 +274,7 @@
     slots = interlace.shape[0]
     tiles = lax.axis_size("depth")
     bricks = lax.axis_size("brick")
+    first = tiles // 2 + 1
     root = (lax.axis_size("tile") // 2 + 1) * bricks + bricks // 2
     order = np.arange(owners, dtype=np.int32)
     order[0], order[root] = root, 0
@@ -286,9 +295,16 @@
     in_front = lax.axis_index("depth") % 2 == 0
     index = jnp.stack([jnp.where(in_front, own, other), jnp.where(in_front, other, own)])
     earlier, target = plan(index, interlace.reshape(1, slots), jnp.asarray(order).reshape(1, owners), capacity)
-    strip = compose_strip(sent.reshape(owners * 8, width), earlier, target, tiles)
-    strips = lax.all_to_all(strip, "depth", split_axis=0, concat_axis=0, tiled=True)
-    return stack(strips).reshape(1, 1, slots // tiles, 4, width)
+    strip = compose_strip(sent.reshape(owners * 8, width), earlier, target, tiles, first)
+    strips = lax.all_to_all(
+        strip,
+        "depth",
+        split_axis=0,
+        concat_axis=0,
+        tiled=True,
+        axis_index_groups=[[place ^ first for place in range(tiles)]],
+    )
+    return stack(strips, first).reshape(1, 1, slots // tiles, 4, width)
 
 
 def solution(mesh):

time: 51.9 us -> 50.4 us (0.971)
  blocking collectives: 11.2 us -> 9.61 us
    all_to_all x1, blocking collectives: 11.2 us -> 9.61 us  [shards(): lax.all_to_all(strip, 'depth', split_axis=0, concat_axis=0, tiled=True, a...]
where the time goes in v4:
time: 50.4 us; the launch traced here: 50.1 us
  starting transfers between devices  26.1 us (52%)
  blocking collectives  9.61 us (19%)
  waiting for transfers between devices  7.3 us (14%)
  Pallas kernels  5.71 us (11%)
  local copies, waits for them, and re-layouts  0.66 us (1%)
  other arithmetic  0.62 us (1%)
    all_to_all x1, starting transfers between devices, shards(): lax.all_to_all(blocks.reshape(2 * owners, 4, width), ('depth', 'tile', 'b...  23.4 us
    all_to_all x1, blocking collectives, shards(): lax.all_to_all(strip, 'depth', split_axis=0, concat_axis=0, tiled=True, a...  9.61 us
    all_to_all x1, waiting for transfers between devices, shards(): lax.all_to_all(blocks.reshape(2 * owners, 4, width), ('depth', 'tile', 'b...  6.51 us
    pallas_call x1, Pallas kernels, blend(): pl.pallas_call(kernel, in_specs=[pl.BlockSpec(memory_space=pl.ANY)] * 3,...  2.84 us
    ppermute x1, starting transfers between devices, shards(): lax.ppermute(own, 'depth', [(place, place ^ 1) for place in range(tiles)])  2.74 us
    pallas_call x1, Pallas kernels, plan(): pl.pallas_call(kernel, out_specs=(pl.BlockSpec(memory_space=pltpu.VMEM),)...  1.32 us
  transfers between devices with their start and end apart: 2, of which 2 were waited for; matrix products, arithmetic and copies ran while one was open for 1% of the time, Pallas kernels for 3%

profile of v4, /device:TPU:1, one launch (start us, length us, event | category | flops | bytes accessed | tf_op | source)
XLA Modules:
  0.0 50.1 jit_solution(16839093971538552857)
XLA Ops:
  0.0 2.8 %blend.1 = f32[512,128]{1,0:T(8,128)} custom-call(f32[2048,128]{1,0:T(8,128)} %bitcast.18, s32[512,128]{1,0:T(8,128)} %bitcast.20, s32[2,64]{1,0:T(2,128)} %bitcast.26), custom_call_target="tpu_custom_call" | custom-call | tf_op jit(solution)/shard_map/blend/pallas_call | solution.py:138
  2.9 0.0 copy-start.2
  2.9 23.4 %all-to-all-start = ((f32[128,4,128]{2,1,0:T(4,128)}), f32[128,4,128]{2,1,0:T(4,128)S(1)}, u32[]{:S(2)}, u32[]{:S(2)}) async-start(f32[128,4,128]{2,1,0:T(4,128)} %bitcast.19), calls=%async_computation | async-start | bytes 524288 | tf_op jit(solution)/shard_map/all_to_all | solution.py:285
  26.2 0.0 copy-start
  26.2 0.0 copy-start.1
  26.2 0.0 copy-done.2
  26.3 0.6 %copy-done = s32[1,1,64,2]{2,3,1,0:T(2,128)S(1)} copy-done((s32[1,1,64,2]{2,3,1,0:T(2,128)S(1)}, s32[1,1,64,2]{2,3,1,0:T(2,128)}, u32[]{:S(2)}) %copy-start) | copy-done | bytes 536
  26.9 0.0 copy-done.1
  26.9 2.7 %collective-permute-start = (s32[4,64]{1,0:T(4,128)S(1)}, s32[4,64]{1,0:T(4,128)S(1)}, u32[]{:S(2)}, u32[]{:S(2)}) collective-permute-start(s32[4,64]{1,0:T(4,128)S(1)} %pad_add_fusion.1), channel_id=1, source_target_pairs={{0,64},{64,0},{128,192},{192,128},{256,320},{320,256},{384,448},{4... | collective-permute-start | bytes 3080 | tf_op jit(solution)/shard_map/ppermute | solution.py:294
  29.7 0.8 %collective-permute-done = s32[4,64]{1,0:T(4,128)S(1)} collective-permute-done((s32[4,64]{1,0:T(4,128)S(1)}, s32[4,64]{1,0:T(4,128)S(1)}, u32[]{:S(2)}, u32[]{:S(2)}) %collective-permute-start) | collective-permute-done | bytes 1056 | tf_op jit(solution)/shard_map/ppermute | solution.py:294
  30.5 0.6 %pad_add_fusion.refs_0_ = s32[2,4,64]{2,1,0:T(4,128)} fusion(s32[1,4,64]{2,1,0:T(4,128)S(1)} %get-tuple-element.10, s32[1,4,64]{2,1,0:T(4,128)S(1)} %get-tuple-element.9), kind=kLoop, calls=%fused_computation | loop fusion | flops 512 | bytes 4096 | tf_op jit(solution)/shard_map/stack | solution.py:296
  31.1 1.3 %plan.1 = (bf16[128,256]{1,0:T(8,128)(2,1)S(1)}, bf16[256,256]{1,0:T(8,128)(2,1)S(1)}) custom-call(s32[2,4,64]{2,1,0:T(4,128)} %pad_add_fusion.refs_0_, s32[1,256]{1,0:T(1,128)} %bitcast.25, s32[1,64]{1,0:T(1,128)} %constant.29.refs_2_), custom_call_target="tpu_custom_call" | custom-call | tf_op jit(solution)/shard_map/plan/pallas_call | solution.py:190
  32.4 6.5 %all-to-all-done = f32[128,4,128]{2,1,0:T(4,128)S(1)} async-done(((f32[128,4,128]{2,1,0:T(4,128)}), f32[128,4,128]{2,1,0:T(4,128)S(1)}, u32[]{:S(2)}, u32[]{:S(2)}) %all-to-all-start) | async-done | bytes 262176 | tf_op jit(solution)/shard_map/all_to_all | solution.py:285
  38.9 0.7 %strip.1 = f32[8,2,32,128]{3,2,1,0:T(8,128)S(1)} custom-call(f32[512,128]{1,0:T(8,128)S(1)} %bitcast.17, bf16[128,256]{1,0:T(8,128)(2,1)S(1)} %get-tuple-element.7.refs_1_, bf16[256,256]{1,0:T(8,128)(2,1)S(1)} %get-tuple-element.8.refs_2_), custom_call_target="tpu_custom_call" | custom-call | tf_op jit(solution)/shard_map/strip/pallas_call | solution.py:234
  39.7 9.6 %all_to_all.10.refs_0_ = f32[8,2,32,128]{3,2,1,0:T(8,128)S(1)} all-to-all(f32[8,2,32,128]{3,2,1,0:T(8,128)S(1)} %strip.1), channel_id=1, replica_groups={{320,256,448,384,64,0,192,128},{321,257,449,385,65,1,193,129},{322,258,..., dimensions={0} | all-to-all | bytes 524288 | tf_op jit(solution)/shard_map/all_to_all | solution.py:299
  49.3 0.8 %stack.13 = f32[128,128]{1,0:T(8,128)} custom-call(f32[8,2,32,128]{3,2,1,0:T(8,128)S(1)} %all_to_all.10.refs_0_), custom_call_target="tpu_custom_call" | custom-call | tf_op jit(solution)/shard_map/stack/pallas_call | solution.py:264
  (2 shorter events, 0.0 us)
Async XLA Ops:
  2.9 23.4 %copy-start.2 = (s32[1,1,64]{2,1,0:T(1,128)S(1)}, s32[1,1,64]{2,1,0:T(1,128)}, u32[]{:S(2)}) copy-start(s32[1,1,64]{2,1,0:T(1,128)} %param.11) | copy-start | bytes 772
  2.9 36.1 %all-to-all-start = ((f32[128,4,128]{2,1,0:T(4,128)}), f32[128,4,128]{2,1,0:T(4,128)S(1)}, u32[]{:S(2)}, u32[]{:S(2)}) async-start(f32[128,4,128]{2,1,0:T(4,128)} %bitcast.19), calls=%async_computation | async-start | bytes 524288 | tf_op jit(solution)/shard_map/all_to_all | solution.py:285
  26.2 0.7 %copy-start = (s32[1,1,64,2]{2,3,1,0:T(2,128)S(1)}, s32[1,1,64,2]{2,3,1,0:T(2,128)}, u32[]{:S(2)}) copy-start(s32[1,1,64,2]{2,3,1,0:T(2,128)} %param.12) | copy-start | bytes 1540
  26.2 0.7 %copy-start.1 = (s32[1,64]{1,0:T(1,128)S(1)}, s32[1,64]{1,0:T(1,128)}, u32[]{:S(2)}) copy-start(s32[1,64]{1,0:T(1,128)} %param.13) | copy-start | bytes 772
  26.9 3.5 %collective-permute-start = (s32[4,64]{1,0:T(4,128)S(1)}, s32[4,64]{1,0:T(4,128)S(1)}, u32[]{:S(2)}, u32[]{:S(2)}) collective-permute-start(s32[4,64]{1,0:T(4,128)S(1)} %pad_add_fusion.1), channel_id=1, source_target_pairs={{0,64},{64,0},{128,192},{192,128},{256,320},{320,256},{384,448},{4... | collective-permute-start | bytes 3080 | tf_op jit(solution)/shard_map/ppermute | solution.py:294

commit v5 on v4

v5 whole, which is shorter than its diff:
```python
import jax
import jax.numpy as jnp
import numpy as np
from jax import lax
from jax.experimental import pallas as pl
from jax.experimental.pallas import tpu as pltpu
from jax.sharding import PartitionSpec as P


def resident(array):
    return pltpu.with_memory_space_constraint(array, pltpu.VMEM)


def columns(row, rows, width):
    length = row.shape[1]
    place = lax.broadcasted_iota(jnp.int32, (rows, length), 1)
    own = lax.broadcasted_iota(jnp.int32, (rows, length), 0)
    spread = jnp.where(place == own, row.astype(jnp.float32), 0.0).astype(jnp.bfloat16)
    return jnp.dot(spread, jnp.ones((length, width), jnp.bfloat16), preferred_element_type=jnp.float32)


def reorder(row, order):
    length = row.shape[1]
    source = lax.broadcasted_iota(jnp.int32, (length, length), 0)
    chosen = jnp.where(source == order, 1.0, 0.0).astype(jnp.bfloat16)
    rows = jnp.broadcast_to(row.astype(jnp.float32), (8, length)).astype(jnp.bfloat16)
    return jnp.dot(rows, chosen, preferred_element_type=jnp.float32)[0:1, :].astype(jnp.int32)


def halves(values):
    high = values.astype(jnp.bfloat16)
    low = (values - high.astype(jnp.float32)).astype(jnp.bfloat16)
    return high, low


def picked(matrix, values):
    return jnp.dot(matrix, jnp.concatenate(halves(values), axis=0), preferred_element_type=jnp.float32)


def turned(values):
    return pltpu.roll(values, values.shape[-1] // 2, values.ndim - 1)


def in_left(values):
    lane = lax.broadcasted_iota(jnp.int32, values.shape, values.ndim - 1)
    return lane < values.shape[-1] // 2


def lefts(one, two):
    return jnp.where(in_left(one), one, turned(two))


def rights(one, two):
    return jnp.where(in_left(one), turned(one), two)


def blend_kernel(root, fragments, ranks, counts, out, pixels, layers, counted, mixed, *sems):
    capacity, owners = counts.shape
    width = out.shape[1]
    share = owners // 2
    pitch = pixels.shape[0] // owners
    wide = share * capacity * 4

    def fetched(step):
        rows = pl.ds(step * share, share)
        place = pixels.reshape(owners, pitch, width).at[rows, pl.ds(0, capacity * 16)]
        return pltpu.make_async_copy(fragments.at[rows], place, sems[0].at[step])

    def stored(step):
        rows = pl.ds((1 - step) * wide, wide)
        return pltpu.make_async_copy(mixed.at[rows], out.at[rows], sems[1].at[step])

    rank_copy = pltpu.make_async_copy(ranks, layers, sems[2])
    count_copy = pltpu.make_async_copy(counts, counted, sems[3])
    fetched(1).start()
    rank_copy.start()
    count_copy.start()
    fetched(0).start()
    pixel = lax.broadcasted_iota(jnp.int32, (owners, width), 1).astype(jnp.float32)
    visible = None
    for step in (1, 0):
        if visible is None:
            rank_copy.wait()
            count_copy.wait()
            visible = [
                jnp.where(pixel < columns(counted[slot : slot + 1, :], owners, width), 1.0, 0.0)
                for slot in range(capacity)
            ]
        fetched(step).wait()
        blended = []
        for slot in range(capacity):
            rank = [
                layers[pl.ds(step * wide + slot * 4 + layer, share, stride=capacity * 4), :] for layer in range(4)
            ]
            entry = [
                [
                    pixels[pl.ds(step * share * pitch + slot * 16 + layer * 4 + part, share, stride=pitch), :]
                    for part in range(4)
                ]
                for layer in range(4)
            ]
            clear = [1.0 - entry[layer][3] for layer in range(4)]
            weight = [visible[slot][step * share : (step + 1) * share]] * 4
            for one in range(4):
                for two in range(one + 1, 4):
                    ahead = rank[one] < rank[two]
                    weight[two] = weight[two] * jnp.where(ahead, clear[one], 1.0)
                    weight[one] = weight[one] * jnp.where(ahead, 1.0, clear[two])
            blended.append([])
            for part in range(4):
                total = entry[0][part] * weight[0]
                for layer in range(1, 4):
                    total = total + entry[layer][part] * weight[layer]
                blended[slot].append(total)
        base = (1 - step) * wide
        for part in range(4):
            one, two = blended[0][part], blended[1][part]
            mixed[pl.ds(base + part, share, stride=4), :] = rights(one, two)
            mixed[pl.ds(base + wide // 2 + part, share, stride=4), :] = lefts(one, two)
        if step == 1:
            for half in range(2):
                first = pl.ds(half * wide // 2, 4)
                other = pl.ds(half * wide // 2 + (root - share) * 4, 4)
                moved = mixed[first, :]
                mixed[first, :] = mixed[other, :]
                mixed[other, :] = moved
        stored(step).start()
    for step in (1, 0):
        stored(step).wait()


def blend(fragments, ranks, counts, root):
    owners, capacity, _, width = fragments.shape
    rows = owners * capacity

    def kernel(*refs):
        blend_kernel(root, *refs)

    return pl.pallas_call(
        kernel,
        in_specs=[pl.BlockSpec(memory_space=pl.ANY)] * 3,
        out_specs=pl.BlockSpec(memory_space=pl.ANY),
        out_shape=jax.ShapeDtypeStruct((rows * 4, width), jnp.float32),
        scratch_shapes=[
            pltpu.VMEM((owners * (capacity * 16 + 8), width), jnp.float32),
            pltpu.VMEM((rows * 4, width), jnp.int32),
            pltpu.VMEM((capacity, owners), jnp.int32),
            pltpu.VMEM((rows * 4, width), jnp.float32),
            pltpu.SemaphoreType.DMA((2,)),
            pltpu.SemaphoreType.DMA((2,)),
            pltpu.SemaphoreType.DMA,
            pltpu.SemaphoreType.DMA,
        ],
        name="blend",
    )(fragments.reshape(owners, capacity * 16, width), ranks.reshape(rows * 4, width), counts)


def plan_kernel(capacity, tiles, index, interlace, placed, earlier, plain, crossed):
    bricks = placed.shape[1]
    slots = interlace.shape[1]
    total = capacity * bricks
    place = placed[...]
    gap = slots // tiles // 2
    row = lax.broadcasted_iota(jnp.int32, (slots // 2, total), 0)
    near = row + row // gap * gap

    def store(target, slab, chosen):
        ones = jnp.where(chosen, 1.0, 0.0).astype(jnp.bfloat16)
        rows = ones.shape[0]
        target[slab * rows : (slab + 1) * rows, :] = jnp.concatenate([ones, ones], axis=1)

    for slab in range(2):
        count = reorder(index[slab, 0:1, :], place)
        rank = jnp.concatenate([reorder(index[slab, 1:2, :], place)] * capacity, axis=1)
        run = jnp.concatenate(
            [reorder(index[slab, 2 + slot : 3 + slot, :], place) for slot in range(capacity)], axis=1
        )
        live = jnp.concatenate([jnp.where(count > slot, 1, 0) for slot in range(capacity)], axis=1) > 0
        run_of = columns(run, total, total).astype(jnp.int32)
        rank_of = columns(rank, total, total).astype(jnp.int32)
        store(earlier, slab, (run_of == run) & (rank < rank_of) & live)
        slot_id = lax.broadcasted_iota(jnp.int32, (slots, total), 0)
        landing = jnp.where(slot_id == run, 1.0, 0.0).astype(jnp.bfloat16)
        screen = jnp.dot(
            jnp.broadcast_to(interlace[...].astype(jnp.float32), (8, slots)).astype(jnp.bfloat16),
            landing,
            preferred_element_type=jnp.float32,
        )[0:1, :].astype(jnp.int32)
        store((plain, crossed)[slab], slab, (near == screen) & live)
        store((crossed, plain)[slab], slab, (near + gap == screen) & live)


def plan(index, interlace, placed, capacity, tiles):
    total = capacity * placed.shape[1]
    slots = interlace.shape[1]

    def kernel(*refs):
        plan_kernel(capacity, tiles, *refs)

    return pl.pallas_call(
        kernel,
        out_specs=(pl.BlockSpec(memory_space=pltpu.VMEM),) * 3,
        out_shape=(
            pltpu.VMEM((2 * total, 2 * total), jnp.bfloat16),
            pltpu.VMEM((slots, 2 * total), jnp.bfloat16),
            pltpu.VMEM((slots, 2 * total), jnp.bfloat16),
        ),
        name="plan",
    )(index, interlace, placed)


def strip_kernel(first, blocks, earlier, plain, crossed, out):
    tiles, _, share, width = out.shape
    quarter = blocks.shape[0] // 4

    def rows_of(side, part):
        return jnp.concatenate(
            [blocks[pl.ds((2 * run + side) * quarter + part, quarter // 4, stride=4), :] for run in range(2)], axis=0
        )

    def part_of(part):
        front, back = rows_of(1, part), rows_of(0, part)
        return jnp.concatenate([lefts(front, back), rights(front, back)], axis=0)

    def sides(values):
        half = values.shape[0] // 2
        return values[:half], values[half:]

    parts = [part_of(part) for part in range(4)]
    front, back = sides(picked(earlier[...], jnp.log(1.0 - parts[3])))
    passed = jnp.exp(jnp.where(in_left(front), front, back))
    shaded = [part * passed for part in parts]
    here_front, here_back = sides(picked(plain[...], jnp.concatenate(shaded, axis=1)))
    there_front, there_back = sides(picked(crossed[...], jnp.concatenate([turned(part) for part in shaded], axis=1)))
    fronts, backs = [], []
    for part in range(4):
        lanes = slice(part * width, (part + 1) * width)
        left = in_left(here_front[:, lanes])
        fronts.append(jnp.where(left, here_front[:, lanes], there_front[:, lanes]))
        backs.append(jnp.where(left, there_back[:, lanes], here_back[:, lanes]))
    clear = 1.0 - fronts[3]
    for part in range(4):
        merged = fronts[part] + clear * backs[part]
        for tile in range(tiles):
            out[tile ^ first, part] = merged[tile * share : (tile + 1) * share]


def compose_strip(blocks, earlier, plain, crossed, tiles, first):
    width = blocks.shape[1]
    slots = plain.shape[0]

    def kernel(*refs):
        strip_kernel(first, *refs)

    return pl.pallas_call(
        kernel,
        in_specs=[pl.BlockSpec(memory_space=pltpu.VMEM)] * 4,
        out_specs=pl.BlockSpec(memory_space=pltpu.VMEM),
        out_shape=pltpu.VMEM((tiles, 4, slots // tiles // 2, width), jnp.float32),
        name="strip",
    )(resident(blocks), resident(earlier), resident(plain), resident(crossed))


def stack_kernel(first, strips, out):
    slabs, _, share, _ = strips.shape
    totals = []
    for half in range(2):
        total = [strips[(slabs - 2 + half) ^ first, part] for part in range(4)]
        for slab in range(slabs - 4, -1, -2):
            front = [strips[(slab + half) ^ first, part] for part in range(4)]
            clear = 1.0 - front[3]
            total = [front[part] + clear * total[part] for part in range(4)]
        totals.append(total)
    for part in range(4):
        out[pl.ds(part, share, stride=4), :] = lefts(totals[0][part], totals[1][part])
        out[pl.ds(share * 4 + part, share, stride=4), :] = rights(totals[0][part], totals[1][part])


def stack(strips, first):
    _, _, share, width = strips.shape

    def kernel(*refs):
        stack_kernel(first, *refs)

    return pl.pallas_call(
        kernel,
        in_specs=[pl.BlockSpec(memory_space=pltpu.VMEM)],
        out_shape=jax.ShapeDtypeStruct((share * 8, width), jnp.float32),
        name="stack",
    )(resident(strips))


def shards(fragments, layer_rank, pixel_count, slot_count, block_run, brick_order, interlace):
    _, _, owners, capacity, _, width = fragments.shape
    slots = interlace.shape[0]
    tiles = lax.axis_size("depth")
    bricks = lax.axis_size("brick")
    first = tiles // 2 + 1
    root = (lax.axis_size("tile") // 2 + 1) * bricks + bricks // 2
    runs = np.split(np.arange(owners, dtype=np.int32), 2)[::-1]
    runs[0][[0, root - owners // 2]] = runs[0][[root - owners // 2, 0]]
    order = np.concatenate(runs)
    blocks = blend(fragments[0, 0], layer_rank[0, 0], pixel_count[0, 0].T, root)
    groups = [
        [int(owners * (2 * chip + core) + owner) for run in runs for core in (1, 0) for owner in run]
        for chip in range(tiles // 2)
    ]
    sent = lax.all_to_all(
        blocks.reshape(2 * owners, 4, width),
        ("depth", "tile", "brick"),
        split_axis=0,
        concat_axis=0,
        tiled=True,
        axis_index_groups=groups,
    )
    own = jnp.concatenate([slot_count[0], brick_order, block_run[0, 0].T], axis=0)
    other = lax.ppermute(own, "depth", [(place, place ^ 1) for place in range(tiles)])
    in_front = lax.axis_index("depth") % 2 == 0
    index = jnp.stack([jnp.where(in_front, own, other), jnp.where(in_front, other, own)])
    plans = plan(index, interlace.reshape(1, slots), jnp.asarray(order).reshape(1, owners), capacity, tiles)
    strip = compose_strip(sent.reshape(owners * 8, width), *plans, tiles, first)
    strips = lax.all_to_all(
        strip,
        "depth",
        split_axis=0,
        concat_axis=0,
        tiled=True,
        axis_index_groups=[[place ^ first for place in range(tiles)]],
    )
    return stack(strips, first).reshape(1, 1, slots // tiles, 4, width)


def solution(mesh):
    return jax.shard_map(
        shards,
        mesh=mesh,
        in_specs=(
            P("depth", ("tile", "brick"), None, None, None, None),
            P("depth", ("tile", "brick"), None, None, None),
            P("depth", ("tile", "brick"), None, None),
            P("depth", ("tile", "brick"), None),
            P("depth", ("tile", "brick"), None, None),
            P("depth", None),
            P(),
        ),
        out_specs=P(("tile", "brick"), "depth", None, None, None),
        check_vma=False,
    )
```

time: 50.4 us -> 49.9 us (0.990)
  Pallas kernels: 5.71 us -> 4.98 us
    pallas_call x1, Pallas kernels: 2.84 us -> 2.32 us  [blend(): pl.pallas_call(kernel, in_specs=[pl.BlockSpec(memory_space=pl.ANY)] * 3,...]
where the time goes in v5:
time: 49.9 us; the launch traced here: 49.6 us
  starting transfers between devices  26.1 us (52%)
  blocking collectives  9.61 us (19%)
  waiting for transfers between devices  7.6 us (15%)
  Pallas kernels  4.98 us (10%)
  local copies, waits for them, and re-layouts  0.66 us (1%)
  other arithmetic  0.62 us (1%)
    all_to_all x1, starting transfers between devices, shards(): lax.all_to_all(blocks.reshape(2 * owners, 4, width), ('depth', 'tile', 'b...  23.5 us
    all_to_all x1, blocking collectives, shards(): lax.all_to_all(strip, 'depth', split_axis=0, concat_axis=0, tiled=True, a...  9.61 us
    all_to_all x1, waiting for transfers between devices, shards(): lax.all_to_all(blocks.reshape(2 * owners, 4, width), ('depth', 'tile', 'b...  6.81 us
    ppermute x1, starting transfers between devices, shards(): lax.ppermute(own, 'depth', [(place, place ^ 1) for place in range(tiles)])  2.52 us
    pallas_call x1, Pallas kernels, blend(): pl.pallas_call(kernel, in_specs=[pl.BlockSpec(memory_space=pl.ANY)] * 3,...  2.32 us
    pallas_call x1, Pallas kernels, plan(): pl.pallas_call(kernel, out_specs=(pl.BlockSpec(memory_space=pltpu.VMEM),)...  1.31 us
  transfers between devices with their start and end apart: 2, of which 2 were waited for; matrix products, arithmetic and copies ran while one was open for 1% of the time, Pallas kernels for 3%

profile of v5, /device:TPU:1, one launch (start us, length us, event | category | flops | bytes accessed | tf_op | source)
XLA Modules:
  0.0 49.6 jit_solution(1355826857363997606)
XLA Ops:
  0.0 2.3 %blend.1 = f32[512,128]{1,0:T(8,128)} custom-call(f32[64,32,128]{2,1,0:T(8,128)} %bitcast.18, s32[512,128]{1,0:T(8,128)} %bitcast.20, s32[2,64]{1,0:T(2,128)} %bitcast.26), custom_call_target="tpu_custom_call" | custom-call | tf_op jit(solution)/shard_map/blend/pallas_call | solution.py:139
  2.3 0.0 copy-start.2
  2.3 23.5 %all-to-all-start = ((f32[128,4,128]{2,1,0:T(4,128)}), f32[128,4,128]{2,1,0:T(4,128)S(1)}, u32[]{:S(2)}, u32[]{:S(2)}) async-start(f32[128,4,128]{2,1,0:T(4,128)} %bitcast.19), calls=%async_computation | async-start | bytes 524288 | tf_op jit(solution)/shard_map/all_to_all | solution.py:308
  25.9 0.0 copy-start
  25.9 0.0 copy-start.1
  25.9 0.0 copy-done.2
  25.9 0.6 %copy-done = s32[1,1,64,2]{2,3,1,0:T(2,128)S(1)} copy-done((s32[1,1,64,2]{2,3,1,0:T(2,128)S(1)}, s32[1,1,64,2]{2,3,1,0:T(2,128)}, u32[]{:S(2)}) %copy-start) | copy-done | bytes 536
  26.6 0.0 copy-done.1
  26.6 2.5 %collective-permute-start = (s32[4,64]{1,0:T(4,128)S(1)}, s32[4,64]{1,0:T(4,128)S(1)}, u32[]{:S(2)}, u32[]{:S(2)}) collective-permute-start(s32[4,64]{1,0:T(4,128)S(1)} %pad_add_fusion.1), channel_id=1, source_target_pairs={{0,64},{64,0},{128,192},{192,128},{256,320},{320,256},{384,448},{4... | collective-permute-start | bytes 3080 | tf_op jit(solution)/shard_map/ppermute | solution.py:317
  29.1 0.8 %collective-permute-done = s32[4,64]{1,0:T(4,128)S(1)} collective-permute-done((s32[4,64]{1,0:T(4,128)S(1)}, s32[4,64]{1,0:T(4,128)S(1)}, u32[]{:S(2)}, u32[]{:S(2)}) %collective-permute-start) | collective-permute-done | bytes 1056 | tf_op jit(solution)/shard_map/ppermute | solution.py:317
  29.9 0.6 %pad_add_fusion.refs_0_ = s32[2,4,64]{2,1,0:T(4,128)} fusion(s32[1,4,64]{2,1,0:T(4,128)S(1)} %get-tuple-element.12, s32[1,4,64]{2,1,0:T(4,128)S(1)} %get-tuple-element.11), kind=kLoop, calls=%fused_computation | loop fusion | flops 512 | bytes 4096 | tf_op jit(solution)/shard_map/stack | solution.py:319
  30.5 1.3 %plan.1 = (bf16[256,256]{1,0:T(8,128)(2,1)S(1)}, bf16[256,256]{1,0:T(8,128)(2,1)S(1)}, bf16[256,256]{1,0:T(8,128)(2,1)S(1)}) custom-call(s32[2,4,64]{2,1,0:T(4,128)} %pad_add_fusion.refs_0_, s32[1,256]{1,0:T(1,128)} %bitcast.25, s32[1,64]{1,0:T(1,128)} %constant.29.refs_2_), custom_call_target="tpu_custom_call" | custom-call | tf_op jit(solution)/shard_map/plan/pallas_call | solution.py:200
  31.8 6.8 %all-to-all-done = f32[128,4,128]{2,1,0:T(4,128)S(1)} async-done(((f32[128,4,128]{2,1,0:T(4,128)}), f32[128,4,128]{2,1,0:T(4,128)S(1)}, u32[]{:S(2)}, u32[]{:S(2)}) %all-to-all-start) | async-done | bytes 262176 | tf_op jit(solution)/shard_map/all_to_all | solution.py:308
  38.7 0.6 %strip.1 = f32[8,4,16,128]{3,2,1,0:T(8,128)S(1)} custom-call(f32[512,128]{1,0:T(8,128)S(1)} %bitcast.17, bf16[256,256]{1,0:T(8,128)(2,1)S(1)} %get-tuple-element.8.refs_1_, bf16[256,256]{1,0:T(8,128)(2,1)S(1)} %get-tuple-element.9.refs_2_, bf16[256,256]{1,0:T(8,128)(2,1)S(1)} %get-tuple-element.10.refs_3_), custom_call_target="tpu_custom_call" | custom-call | tf_op jit(solution)/shard_map/strip/pallas_call | solution.py:255
  39.3 9.6 %all_to_all.10.refs_0_ = f32[8,4,16,128]{3,2,1,0:T(8,128)S(1)} all-to-all(f32[8,4,16,128]{3,2,1,0:T(8,128)S(1)} %strip.1), channel_id=1, replica_groups={{320,256,448,384,64,0,192,128},{321,257,449,385,65,1,193,129},{322,258,..., dimensions={0} | all-to-all | bytes 524288 | tf_op jit(solution)/shard_map/all_to_all | solution.py:322
  48.9 0.7 %stack.13 = f32[128,128]{1,0:T(8,128)} custom-call(f32[8,4,16,128]{3,2,1,0:T(8,128)S(1)} %all_to_all.10.refs_0_), custom_call_target="tpu_custom_call" | custom-call | tf_op jit(solution)/shard_map/stack/pallas_call | solution.py:285
  (2 shorter events, 0.0 us)
Async XLA Ops:
  2.3 23.6 %copy-start.2 = (s32[1,1,64]{2,1,0:T(1,128)S(1)}, s32[1,1,64]{2,1,0:T(1,128)}, u32[]{:S(2)}) copy-start(s32[1,1,64]{2,1,0:T(1,128)} %param.11) | copy-start | bytes 772
  2.3 36.3 %all-to-all-start = ((f32[128,4,128]{2,1,0:T(4,128)}), f32[128,4,128]{2,1,0:T(4,128)S(1)}, u32[]{:S(2)}, u32[]{:S(2)}) async-start(f32[128,4,128]{2,1,0:T(4,128)} %bitcast.19), calls=%async_computation | async-start | bytes 524288 | tf_op jit(solution)/shard_map/all_to_all | solution.py:308
  25.9 0.7 %copy-start = (s32[1,1,64,2]{2,3,1,0:T(2,128)S(1)}, s32[1,1,64,2]{2,3,1,0:T(2,128)}, u32[]{:S(2)}) copy-start(s32[1,1,64,2]{2,3,1,0:T(2,128)} %param.12) | copy-start | bytes 1540
  25.9 0.7 %copy-start.1 = (s32[1,64]{1,0:T(1,128)S(1)}, s32[1,64]{1,0:T(1,128)}, u32[]{:S(2)}) copy-start(s32[1,64]{1,0:T(1,128)} %param.13) | copy-start | bytes 772
  26.6 3.3 %collective-permute-start = (s32[4,64]{1,0:T(4,128)S(1)}, s32[4,64]{1,0:T(4,128)S(1)}, u32[]{:S(2)}, u32[]{:S(2)}) collective-permute-start(s32[4,64]{1,0:T(4,128)S(1)} %pad_add_fusion.1), channel_id=1, source_target_pairs={{0,64},{64,0},{128,192},{192,128},{256,320},{320,256},{384,448},{4... | collective-permute-start | bytes 3080 | tf_op jit(solution)/shard_map/ppermute | solution.py:317

commit v6 on v5

--- a/solution.py
+++ b/solution.py
@@ -220,18 +220,23 @@
 
     def part_of(part):
         front, back = rows_of(1, part), rows_of(0, part)
-        return jnp.concatenate([lefts(front, back), rights(front, back)], axis=0)
+        left, front_turned, back_turned = in_left(front), turned(front), turned(back)
+        plain_rows = [jnp.where(left, front, back_turned), jnp.where(left, front_turned, back)]
+        crossed_rows = [jnp.where(left, back, front_turned), jnp.where(left, back_turned, front)]
+        return jnp.concatenate(plain_rows, axis=0), jnp.concatenate(crossed_rows, axis=0)
 
     def sides(values):
         half = values.shape[0] // 2
         return values[:half], values[half:]
 
     parts = [part_of(part) for part in range(4)]
-    front, back = sides(picked(earlier[...], jnp.log(1.0 - parts[3])))
+    front, back = sides(picked(earlier[...], jnp.log(1.0 - parts[3][0])))
     passed = jnp.exp(jnp.where(in_left(front), front, back))
-    shaded = [part * passed for part in parts]
-    here_front, here_back = sides(picked(plain[...], jnp.concatenate(shaded, axis=1)))
-    there_front, there_back = sides(picked(crossed[...], jnp.concatenate([turned(part) for part in shaded], axis=1)))
+    here = jnp.concatenate([part[0] * passed for part in parts], axis=1)
+    here_front, here_back = sides(picked(plain[...], here))
+    passed = turned(passed)
+    there = jnp.concatenate([part[1] * passed for part in parts], axis=1)
+    there_front, there_back = sides(picked(crossed[...], there))
     fronts, backs = [], []
     for part in range(4):
         lanes = slice(part * width, (part + 1) * width)

time: 49.9 us -> 49.8 us (level)
  no operation moved by 1% of the time
where the time goes in v6:
time: 49.8 us; the launch traced here: 49.6 us
  starting transfers between devices  26.1 us (52%)
  blocking collectives  9.61 us (19%)
  waiting for transfers between devices  7.6 us (15%)
  Pallas kernels  4.92 us (10%)
  local copies, waits for them, and re-layouts  0.66 us (1%)
  other arithmetic  0.62 us (1%)
    all_to_all x1, starting transfers between devices, shards(): lax.all_to_all(blocks.reshape(2 * owners, 4, width), ('depth', 'tile', 'b...  23.5 us
    all_to_all x1, blocking collectives, shards(): lax.all_to_all(strip, 'depth', split_axis=0, concat_axis=0, tiled=True, a...  9.61 us
    all_to_all x1, waiting for transfers between devices, shards(): lax.all_to_all(blocks.reshape(2 * owners, 4, width), ('depth', 'tile', 'b...  6.81 us
    ppermute x1, starting transfers between devices, shards(): lax.ppermute(own, 'depth', [(place, place ^ 1) for place in range(tiles)])  2.52 us
    pallas_call x1, Pallas kernels, blend(): pl.pallas_call(kernel, in_specs=[pl.BlockSpec(memory_space=pl.ANY)] * 3,...  2.32 us
    pallas_call x1, Pallas kernels, plan(): pl.pallas_call(kernel, out_specs=(pl.BlockSpec(memory_space=pltpu.VMEM),)...  1.31 us
  transfers between devices with their start and end apart: 2, of which 2 were waited for; matrix products, arithmetic and copies ran while one was open for 1% of the time, Pallas kernels for 3%

profile of v6, /device:TPU:1, one launch (start us, length us, event | category | flops | bytes accessed | tf_op | source)
XLA Modules:
  0.0 49.6 jit_solution(6062717657011424982)
XLA Ops:
  0.0 2.3 %blend.1 = f32[512,128]{1,0:T(8,128)} custom-call(f32[64,32,128]{2,1,0:T(8,128)} %bitcast.18, s32[512,128]{1,0:T(8,128)} %bitcast.20, s32[2,64]{1,0:T(2,128)} %bitcast.26), custom_call_target="tpu_custom_call" | custom-call | tf_op jit(solution)/shard_map/blend/pallas_call | solution.py:139
  2.3 0.0 copy-start.2
  2.3 23.5 %all-to-all-start = ((f32[128,4,128]{2,1,0:T(4,128)}), f32[128,4,128]{2,1,0:T(4,128)S(1)}, u32[]{:S(2)}, u32[]{:S(2)}) async-start(f32[128,4,128]{2,1,0:T(4,128)} %bitcast.19), calls=%async_computation | async-start | bytes 524288 | tf_op jit(solution)/shard_map/all_to_all | solution.py:313
  25.9 0.0 copy-start
  25.9 0.0 copy-start.1
  25.9 0.0 copy-done.2
  25.9 0.6 %copy-done = s32[1,1,64,2]{2,3,1,0:T(2,128)S(1)} copy-done((s32[1,1,64,2]{2,3,1,0:T(2,128)S(1)}, s32[1,1,64,2]{2,3,1,0:T(2,128)}, u32[]{:S(2)}) %copy-start) | copy-done | bytes 536
  26.6 0.0 copy-done.1
  26.6 2.5 %collective-permute-start = (s32[4,64]{1,0:T(4,128)S(1)}, s32[4,64]{1,0:T(4,128)S(1)}, u32[]{:S(2)}, u32[]{:S(2)}) collective-permute-start(s32[4,64]{1,0:T(4,128)S(1)} %pad_add_fusion.1), channel_id=1, source_target_pairs={{0,64},{64,0},{128,192},{192,128},{256,320},{320,256},{384,448},{4... | collective-permute-start | bytes 3080 | tf_op jit(solution)/shard_map/ppermute | solution.py:322
  29.1 0.8 %collective-permute-done = s32[4,64]{1,0:T(4,128)S(1)} collective-permute-done((s32[4,64]{1,0:T(4,128)S(1)}, s32[4,64]{1,0:T(4,128)S(1)}, u32[]{:S(2)}, u32[]{:S(2)}) %collective-permute-start) | collective-permute-done | bytes 1056 | tf_op jit(solution)/shard_map/ppermute | solution.py:322
  29.9 0.6 %pad_add_fusion.refs_0_ = s32[2,4,64]{2,1,0:T(4,128)} fusion(s32[1,4,64]{2,1,0:T(4,128)S(1)} %get-tuple-element.12, s32[1,4,64]{2,1,0:T(4,128)S(1)} %get-tuple-element.11), kind=kLoop, calls=%fused_computation | loop fusion | flops 512 | bytes 4096 | tf_op jit(solution)/shard_map/stack | solution.py:324
  30.5 1.3 %plan.1 = (bf16[256,256]{1,0:T(8,128)(2,1)S(1)}, bf16[256,256]{1,0:T(8,128)(2,1)S(1)}, bf16[256,256]{1,0:T(8,128)(2,1)S(1)}) custom-call(s32[2,4,64]{2,1,0:T(4,128)} %pad_add_fusion.refs_0_, s32[1,256]{1,0:T(1,128)} %bitcast.25, s32[1,64]{1,0:T(1,128)} %constant.29.refs_2_), custom_call_target="tpu_custom_call" | custom-call | tf_op jit(solution)/shard_map/plan/pallas_call | solution.py:200
  31.8 6.8 %all-to-all-done = f32[128,4,128]{2,1,0:T(4,128)S(1)} async-done(((f32[128,4,128]{2,1,0:T(4,128)}), f32[128,4,128]{2,1,0:T(4,128)S(1)}, u32[]{:S(2)}, u32[]{:S(2)}) %all-to-all-start) | async-done | bytes 262176 | tf_op jit(solution)/shard_map/all_to_all | solution.py:313
  38.7 0.6 %strip.1 = f32[8,4,16,128]{3,2,1,0:T(8,128)S(1)} custom-call(f32[512,128]{1,0:T(8,128)S(1)} %bitcast.17, bf16[256,256]{1,0:T(8,128)(2,1)S(1)} %get-tuple-element.8.refs_1_, bf16[256,256]{1,0:T(8,128)(2,1)S(1)} %get-tuple-element.9.refs_2_, bf16[256,256]{1,0:T(8,128)(2,1)S(1)} %get-tuple-element.10.refs_3_), custom_call_target="tpu_custom_call" | custom-call | tf_op jit(solution)/shard_map/strip/pallas_call | solution.py:260
  39.2 9.6 %all_to_all.10.refs_0_ = f32[8,4,16,128]{3,2,1,0:T(8,128)S(1)} all-to-all(f32[8,4,16,128]{3,2,1,0:T(8,128)S(1)} %strip.1), channel_id=1, replica_groups={{320,256,448,384,64,0,192,128},{321,257,449,385,65,1,193,129},{322,258,..., dimensions={0} | all-to-all | bytes 524288 | tf_op jit(solution)/shard_map/all_to_all | solution.py:327
  48.8 0.7 %stack.13 = f32[128,128]{1,0:T(8,128)} custom-call(f32[8,4,16,128]{3,2,1,0:T(8,128)S(1)} %all_to_all.10.refs_0_), custom_call_target="tpu_custom_call" | custom-call | tf_op jit(solution)/shard_map/stack/pallas_call | solution.py:290
  (2 shorter events, 0.0 us)
Async XLA Ops:
  2.3 23.6 %copy-start.2 = (s32[1,1,64]{2,1,0:T(1,128)S(1)}, s32[1,1,64]{2,1,0:T(1,128)}, u32[]{:S(2)}) copy-start(s32[1,1,64]{2,1,0:T(1,128)} %param.11) | copy-start | bytes 772
  2.3 36.3 %all-to-all-start = ((f32[128,4,128]{2,1,0:T(4,128)}), f32[128,4,128]{2,1,0:T(4,128)S(1)}, u32[]{:S(2)}, u32[]{:S(2)}) async-start(f32[128,4,128]{2,1,0:T(4,128)} %bitcast.19), calls=%async_computation | async-start | bytes 524288 | tf_op jit(solution)/shard_map/all_to_all | solution.py:313
  25.9 0.7 %copy-start = (s32[1,1,64,2]{2,3,1,0:T(2,128)S(1)}, s32[1,1,64,2]{2,3,1,0:T(2,128)}, u32[]{:S(2)}) copy-start(s32[1,1,64,2]{2,3,1,0:T(2,128)} %param.12) | copy-start | bytes 1540
  25.9 0.7 %copy-start.1 = (s32[1,64]{1,0:T(1,128)S(1)}, s32[1,64]{1,0:T(1,128)}, u32[]{:S(2)}) copy-start(s32[1,64]{1,0:T(1,128)} %param.13) | copy-start | bytes 772
  26.6 3.3 %collective-permute-start = (s32[4,64]{1,0:T(4,128)S(1)}, s32[4,64]{1,0:T(4,128)S(1)}, u32[]{:S(2)}, u32[]{:S(2)}) collective-permute-start(s32[4,64]{1,0:T(4,128)S(1)} %pad_add_fusion.1), channel_id=1, source_target_pairs={{0,64},{64,0},{128,192},{192,128},{256,320},{320,256},{384,448},{4... | collective-permute-start | bytes 3080 | tf_op jit(solution)/shard_map/ppermute | solution.py:322

commit v7 on v6

--- a/solution.py
+++ b/solution.py
@@ -247,7 +247,7 @@
     for part in range(4):
         merged = fronts[part] + clear * backs[part]
         for tile in range(tiles):
-            out[tile ^ first, part] = merged[tile * share : (tile + 1) * share]
+            out[first.index(tile), part] = merged[tile * share : (tile + 1) * share]
 
 
 def compose_strip(blocks, earlier, plain, crossed, tiles, first):
@@ -270,9 +270,9 @@
     slabs, _, share, _ = strips.shape
     totals = []
     for half in range(2):
-        total = [strips[(slabs - 2 + half) ^ first, part] for part in range(4)]
+        total = [strips[first.index(slabs - 2 + half), part] for part in range(4)]
         for slab in range(slabs - 4, -1, -2):
-            front = [strips[(slab + half) ^ first, part] for part in range(4)]
+            front = [strips[first.index(slab + half), part] for part in range(4)]
             clear = 1.0 - front[3]
             total = [front[part] + clear * total[part] for part in range(4)]
         totals.append(total)
@@ -300,7 +300,8 @@
     slots = interlace.shape[0]
     tiles = lax.axis_size("depth")
     bricks = lax.axis_size("brick")
-    first = tiles // 2 + 1
+    middle = tiles // 2
+    first = [middle + 1, middle, *range(middle + 2, tiles), *range(middle - 2, middle), *range(middle - 2)]
     root = (lax.axis_size("tile") // 2 + 1) * bricks + bricks // 2
     runs = np.split(np.arange(owners, dtype=np.int32), 2)[::-1]
     runs[0][[0, root - owners // 2]] = runs[0][[root - owners // 2, 0]]
@@ -330,7 +331,7 @@
         split_axis=0,
         concat_axis=0,
         tiled=True,
-        axis_index_groups=[[place ^ first for place in range(tiles)]],
+        axis_index_groups=[first],
     )
     return stack(strips, first).reshape(1, 1, slots // tiles, 4, width)
 

time: 49.8 us -> 49.5 us (level)
  no operation moved by 1% of the time
where the time goes in v7:
time: 49.5 us; the launch traced here: 49.3 us
  starting transfers between devices  26.1 us (53%)
  blocking collectives  9.31 us (19%)
  waiting for transfers between devices  7.6 us (15%)
  Pallas kernels  4.92 us (10%)
  local copies, waits for them, and re-layouts  0.66 us (1%)
  other arithmetic  0.62 us (1%)
    all_to_all x1, starting transfers between devices, shards(): lax.all_to_all(blocks.reshape(2 * owners, 4, width), ('depth', 'tile', 'b...  23.5 us
    all_to_all x1, blocking collectives, shards(): lax.all_to_all(strip, 'depth', split_axis=0, concat_axis=0, tiled=True, a...  9.31 us
    all_to_all x1, waiting for transfers between devices, shards(): lax.all_to_all(blocks.reshape(2 * owners, 4, width), ('depth', 'tile', 'b...  6.81 us
    ppermute x1, starting transfers between devices, shards(): lax.ppermute(own, 'depth', [(place, place ^ 1) for place in range(tiles)])  2.52 us
    pallas_call x1, Pallas kernels, blend(): pl.pallas_call(kernel, in_specs=[pl.BlockSpec(memory_space=pl.ANY)] * 3,...  2.32 us
    pallas_call x1, Pallas kernels, plan(): pl.pallas_call(kernel, out_specs=(pl.BlockSpec(memory_space=pltpu.VMEM),)...  1.31 us
  transfers between devices with their start and end apart: 2, of which 2 were waited for; matrix products, arithmetic and copies ran while one was open for 1% of the time, Pallas kernels for 3%

profile of v7, /device:TPU:1, one launch (start us, length us, event | category | flops | bytes accessed | tf_op | source)
XLA Modules:
  0.0 49.3 jit_solution(11593321698146975342)
XLA Ops:
  0.0 2.3 %blend.1 = f32[512,128]{1,0:T(8,128)} custom-call(f32[64,32,128]{2,1,0:T(8,128)} %bitcast.18, s32[512,128]{1,0:T(8,128)} %bitcast.20, s32[2,64]{1,0:T(2,128)} %bitcast.26), custom_call_target="tpu_custom_call" | custom-call | tf_op jit(solution)/shard_map/blend/pallas_call | solution.py:139
  2.3 0.0 copy-start.2
  2.3 23.5 %all-to-all-start = ((f32[128,4,128]{2,1,0:T(4,128)}), f32[128,4,128]{2,1,0:T(4,128)S(1)}, u32[]{:S(2)}, u32[]{:S(2)}) async-start(f32[128,4,128]{2,1,0:T(4,128)} %bitcast.19), calls=%async_computation | async-start | bytes 524288 | tf_op jit(solution)/shard_map/all_to_all | solution.py:314
  25.9 0.0 copy-start
  25.9 0.0 copy-start.1
  25.9 0.0 copy-done.2
  25.9 0.6 %copy-done = s32[1,1,64,2]{2,3,1,0:T(2,128)S(1)} copy-done((s32[1,1,64,2]{2,3,1,0:T(2,128)S(1)}, s32[1,1,64,2]{2,3,1,0:T(2,128)}, u32[]{:S(2)}) %copy-start) | copy-done | bytes 536
  26.6 0.0 copy-done.1
  26.6 2.5 %collective-permute-start = (s32[4,64]{1,0:T(4,128)S(1)}, s32[4,64]{1,0:T(4,128)S(1)}, u32[]{:S(2)}, u32[]{:S(2)}) collective-permute-start(s32[4,64]{1,0:T(4,128)S(1)} %pad_add_fusion.1), channel_id=1, source_target_pairs={{0,64},{64,0},{128,192},{192,128},{256,320},{320,256},{384,448},{4... | collective-permute-start | bytes 3080 | tf_op jit(solution)/shard_map/ppermute | solution.py:323
  29.1 0.8 %collective-permute-done = s32[4,64]{1,0:T(4,128)S(1)} collective-permute-done((s32[4,64]{1,0:T(4,128)S(1)}, s32[4,64]{1,0:T(4,128)S(1)}, u32[]{:S(2)}, u32[]{:S(2)}) %collective-permute-start) | collective-permute-done | bytes 1056 | tf_op jit(solution)/shard_map/ppermute | solution.py:323
  29.9 0.6 %pad_add_fusion.refs_0_ = s32[2,4,64]{2,1,0:T(4,128)} fusion(s32[1,4,64]{2,1,0:T(4,128)S(1)} %get-tuple-element.12, s32[1,4,64]{2,1,0:T(4,128)S(1)} %get-tuple-element.11), kind=kLoop, calls=%fused_computation | loop fusion | flops 512 | bytes 4096 | tf_op jit(solution)/shard_map/stack | solution.py:325
  30.5 1.3 %plan.1 = (bf16[256,256]{1,0:T(8,128)(2,1)S(1)}, bf16[256,256]{1,0:T(8,128)(2,1)S(1)}, bf16[256,256]{1,0:T(8,128)(2,1)S(1)}) custom-call(s32[2,4,64]{2,1,0:T(4,128)} %pad_add_fusion.refs_0_, s32[1,256]{1,0:T(1,128)} %bitcast.25, s32[1,64]{1,0:T(1,128)} %constant.29.refs_2_), custom_call_target="tpu_custom_call" | custom-call | tf_op jit(solution)/shard_map/plan/pallas_call | solution.py:200
  31.8 6.8 %all-to-all-done = f32[128,4,128]{2,1,0:T(4,128)S(1)} async-done(((f32[128,4,128]{2,1,0:T(4,128)}), f32[128,4,128]{2,1,0:T(4,128)S(1)}, u32[]{:S(2)}, u32[]{:S(2)}) %all-to-all-start) | async-done | bytes 262176 | tf_op jit(solution)/shard_map/all_to_all | solution.py:314
  38.7 0.6 %strip.1 = f32[8,4,16,128]{3,2,1,0:T(8,128)S(1)} custom-call(f32[512,128]{1,0:T(8,128)S(1)} %bitcast.17, bf16[256,256]{1,0:T(8,128)(2,1)S(1)} %get-tuple-element.8.refs_1_, bf16[256,256]{1,0:T(8,128)(2,1)S(1)} %get-tuple-element.9.refs_2_, bf16[256,256]{1,0:T(8,128)(2,1)S(1)} %get-tuple-element.10.refs_3_), custom_call_target="tpu_custom_call" | custom-call | tf_op jit(solution)/shard_map/strip/pallas_call | solution.py:260
  39.2 9.3 %all_to_all.10.refs_0_ = f32[8,4,16,128]{3,2,1,0:T(8,128)S(1)} all-to-all(f32[8,4,16,128]{3,2,1,0:T(8,128)S(1)} %strip.1), channel_id=1, replica_groups={{320,256,384,448,128,192,0,64},{321,257,385,449,129,193,1,65},{322,258,..., dimensions={0} | all-to-all | bytes 524288 | tf_op jit(solution)/shard_map/all_to_all | solution.py:328
  48.5 0.7 %stack.13 = f32[128,128]{1,0:T(8,128)} custom-call(f32[8,4,16,128]{3,2,1,0:T(8,128)S(1)} %all_to_all.10.refs_0_), custom_call_target="tpu_custom_call" | custom-call | tf_op jit(solution)/shard_map/stack/pallas_call | solution.py:290
  (2 shorter events, 0.0 us)
Async XLA Ops:
  2.3 23.6 %copy-start.2 = (s32[1,1,64]{2,1,0:T(1,128)S(1)}, s32[1,1,64]{2,1,0:T(1,128)}, u32[]{:S(2)}) copy-start(s32[1,1,64]{2,1,0:T(1,128)} %param.11) | copy-start | bytes 772
  2.3 36.3 %all-to-all-start = ((f32[128,4,128]{2,1,0:T(4,128)}), f32[128,4,128]{2,1,0:T(4,128)S(1)}, u32[]{:S(2)}, u32[]{:S(2)}) async-start(f32[128,4,128]{2,1,0:T(4,128)} %bitcast.19), calls=%async_computation | async-start | bytes 524288 | tf_op jit(solution)/shard_map/all_to_all | solution.py:314
  25.9 0.7 %copy-start = (s32[1,1,64,2]{2,3,1,0:T(2,128)S(1)}, s32[1,1,64,2]{2,3,1,0:T(2,128)}, u32[]{:S(2)}) copy-start(s32[1,1,64,2]{2,3,1,0:T(2,128)} %param.12) | copy-start | bytes 1540
  25.9 0.7 %copy-start.1 = (s32[1,64]{1,0:T(1,128)S(1)}, s32[1,64]{1,0:T(1,128)}, u32[]{:S(2)}) copy-start(s32[1,64]{1,0:T(1,128)} %param.13) | copy-start | bytes 772
  26.6 3.3 %collective-permute-start = (s32[4,64]{1,0:T(4,128)S(1)}, s32[4,64]{1,0:T(4,128)S(1)}, u32[]{:S(2)}, u32[]{:S(2)}) collective-permute-start(s32[4,64]{1,0:T(4,128)S(1)} %pad_add_fusion.1), channel_id=1, source_target_pairs={{0,64},{64,0},{128,192},{192,128},{256,320},{320,256},{384,448},{4... | collective-permute-start | bytes 3080 | tf_op jit(solution)/shard_map/ppermute | solution.py:323

commit v8 on v7

--- a/solution.py
+++ b/solution.py
@@ -72,10 +72,10 @@
 
     rank_copy = pltpu.make_async_copy(ranks, layers, sems[2])
     count_copy = pltpu.make_async_copy(counts, counted, sems[3])
+    rank_copy.start()
     fetched(1).start()
-    rank_copy.start()
+    fetched(0).start()
     count_copy.start()
-    fetched(0).start()
     pixel = lax.broadcasted_iota(jnp.int32, (owners, width), 1).astype(jnp.float32)
     visible = None
     for step in (1, 0):

time: 49.5 us -> 49.5 us (level)
  no operation moved by 1% of the time
where the time goes in v8:
time: 49.5 us; the launch traced here: 49.3 us
  starting transfers between devices  26.1 us (53%)
  blocking collectives  9.31 us (19%)
  waiting for transfers between devices  7.6 us (15%)
  Pallas kernels  4.92 us (10%)
  local copies, waits for them, and re-layouts  0.66 us (1%)
  other arithmetic  0.62 us (1%)
    all_to_all x1, starting transfers between devices, shards(): lax.all_to_all(blocks.reshape(2 * owners, 4, width), ('depth', 'tile', 'b...  23.5 us
    all_to_all x1, blocking collectives, shards(): lax.all_to_all(strip, 'depth', split_axis=0, concat_axis=0, tiled=True, a...  9.31 us
    all_to_all x1, waiting for transfers between devices, shards(): lax.all_to_all(blocks.reshape(2 * owners, 4, width), ('depth', 'tile', 'b...  6.81 us
    ppermute x1, starting transfers between devices, shards(): lax.ppermute(own, 'depth', [(place, place ^ 1) for place in range(tiles)])  2.52 us
    pallas_call x1, Pallas kernels, blend(): pl.pallas_call(kernel, in_specs=[pl.BlockSpec(memory_space=pl.ANY)] * 3,...  2.32 us
    pallas_call x1, Pallas kernels, plan(): pl.pallas_call(kernel, out_specs=(pl.BlockSpec(memory_space=pltpu.VMEM),)...  1.31 us
  transfers between devices with their start and end apart: 2, of which 2 were waited for; matrix products, arithmetic and copies ran while one was open for 1% of the time, Pallas kernels for 3%

profile of v8, /device:TPU:1, one launch (start us, length us, event | category | flops | bytes accessed | tf_op | source)
XLA Modules:
  0.0 49.3 jit_solution(3390341701335776164)
XLA Ops:
  0.0 2.3 %blend.1 = f32[512,128]{1,0:T(8,128)} custom-call(f32[64,32,128]{2,1,0:T(8,128)} %bitcast.18, s32[512,128]{1,0:T(8,128)} %bitcast.20, s32[2,64]{1,0:T(2,128)} %bitcast.26), custom_call_target="tpu_custom_call" | custom-call | tf_op jit(solution)/shard_map/blend/pallas_call | solution.py:139
  2.3 0.0 copy-start.2
  2.3 23.5 %all-to-all-start = ((f32[128,4,128]{2,1,0:T(4,128)}), f32[128,4,128]{2,1,0:T(4,128)S(1)}, u32[]{:S(2)}, u32[]{:S(2)}) async-start(f32[128,4,128]{2,1,0:T(4,128)} %bitcast.19), calls=%async_computation | async-start | bytes 524288 | tf_op jit(solution)/shard_map/all_to_all | solution.py:314
  25.9 0.0 copy-start
  25.9 0.0 copy-start.1
  25.9 0.0 copy-done.2
  25.9 0.6 %copy-done = s32[1,1,64,2]{2,3,1,0:T(2,128)S(1)} copy-done((s32[1,1,64,2]{2,3,1,0:T(2,128)S(1)}, s32[1,1,64,2]{2,3,1,0:T(2,128)}, u32[]{:S(2)}) %copy-start) | copy-done | bytes 536
  26.6 0.0 copy-done.1
  26.6 2.5 %collective-permute-start = (s32[4,64]{1,0:T(4,128)S(1)}, s32[4,64]{1,0:T(4,128)S(1)}, u32[]{:S(2)}, u32[]{:S(2)}) collective-permute-start(s32[4,64]{1,0:T(4,128)S(1)} %pad_add_fusion.1), channel_id=1, source_target_pairs={{0,64},{64,0},{128,192},{192,128},{256,320},{320,256},{384,448},{4... | collective-permute-start | bytes 3080 | tf_op jit(solution)/shard_map/ppermute | solution.py:323
  29.1 0.8 %collective-permute-done = s32[4,64]{1,0:T(4,128)S(1)} collective-permute-done((s32[4,64]{1,0:T(4,128)S(1)}, s32[4,64]{1,0:T(4,128)S(1)}, u32[]{:S(2)}, u32[]{:S(2)}) %collective-permute-start) | collective-permute-done | bytes 1056 | tf_op jit(solution)/shard_map/ppermute | solution.py:323
  29.9 0.6 %pad_add_fusion.refs_0_ = s32[2,4,64]{2,1,0:T(4,128)} fusion(s32[1,4,64]{2,1,0:T(4,128)S(1)} %get-tuple-element.12, s32[1,4,64]{2,1,0:T(4,128)S(1)} %get-tuple-element.11), kind=kLoop, calls=%fused_computation | loop fusion | flops 512 | bytes 4096 | tf_op jit(solution)/shard_map/stack | solution.py:325
  30.5 1.3 %plan.1 = (bf16[256,256]{1,0:T(8,128)(2,1)S(1)}, bf16[256,256]{1,0:T(8,128)(2,1)S(1)}, bf16[256,256]{1,0:T(8,128)(2,1)S(1)}) custom-call(s32[2,4,64]{2,1,0:T(4,128)} %pad_add_fusion.refs_0_, s32[1,256]{1,0:T(1,128)} %bitcast.25, s32[1,64]{1,0:T(1,128)} %constant.29.refs_2_), custom_call_target="tpu_custom_call" | custom-call | tf_op jit(solution)/shard_map/plan/pallas_call | solution.py:200
  31.8 6.8 %all-to-all-done = f32[128,4,128]{2,1,0:T(4,128)S(1)} async-done(((f32[128,4,128]{2,1,0:T(4,128)}), f32[128,4,128]{2,1,0:T(4,128)S(1)}, u32[]{:S(2)}, u32[]{:S(2)}) %all-to-all-start) | async-done | bytes 262176 | tf_op jit(solution)/shard_map/all_to_all | solution.py:314
  38.7 0.6 %strip.1 = f32[8,4,16,128]{3,2,1,0:T(8,128)S(1)} custom-call(f32[512,128]{1,0:T(8,128)S(1)} %bitcast.17, bf16[256,256]{1,0:T(8,128)(2,1)S(1)} %get-tuple-element.8.refs_1_, bf16[256,256]{1,0:T(8,128)(2,1)S(1)} %get-tuple-element.9.refs_2_, bf16[256,256]{1,0:T(8,128)(2,1)S(1)} %get-tuple-element.10.refs_3_), custom_call_target="tpu_custom_call" | custom-call | tf_op jit(solution)/shard_map/strip/pallas_call | solution.py:260
  39.2 9.3 %all_to_all.10.refs_0_ = f32[8,4,16,128]{3,2,1,0:T(8,128)S(1)} all-to-all(f32[8,4,16,128]{3,2,1,0:T(8,128)S(1)} %strip.1), channel_id=1, replica_groups={{320,256,384,448,128,192,0,64},{321,257,385,449,129,193,1,65},{322,258,..., dimensions={0} | all-to-all | bytes 524288 | tf_op jit(solution)/shard_map/all_to_all | solution.py:328
  48.5 0.7 %stack.13 = f32[128,128]{1,0:T(8,128)} custom-call(f32[8,4,16,128]{3,2,1,0:T(8,128)S(1)} %all_to_all.10.refs_0_), custom_call_target="tpu_custom_call" | custom-call | tf_op jit(solution)/shard_map/stack/pallas_call | solution.py:290
  (2 shorter events, 0.0 us)
Async XLA Ops:
  2.3 23.6 %copy-start.2 = (s32[1,1,64]{2,1,0:T(1,128)S(1)}, s32[1,1,64]{2,1,0:T(1,128)}, u32[]{:S(2)}) copy-start(s32[1,1,64]{2,1,0:T(1,128)} %param.11) | copy-start | bytes 772
  2.3 36.3 %all-to-all-start = ((f32[128,4,128]{2,1,0:T(4,128)}), f32[128,4,128]{2,1,0:T(4,128)S(1)}, u32[]{:S(2)}, u32[]{:S(2)}) async-start(f32[128,4,128]{2,1,0:T(4,128)} %bitcast.19), calls=%async_computation | async-start | bytes 524288 | tf_op jit(solution)/shard_map/all_to_all | solution.py:314
  25.9 0.7 %copy-start = (s32[1,1,64,2]{2,3,1,0:T(2,128)S(1)}, s32[1,1,64,2]{2,3,1,0:T(2,128)}, u32[]{:S(2)}) copy-start(s32[1,1,64,2]{2,3,1,0:T(2,128)} %param.12) | copy-start | bytes 1540
  25.9 0.7 %copy-start.1 = (s32[1,64]{1,0:T(1,128)S(1)}, s32[1,64]{1,0:T(1,128)}, u32[]{:S(2)}) copy-start(s32[1,64]{1,0:T(1,128)} %param.13) | copy-start | bytes 772
  26.6 3.3 %collective-permute-start = (s32[4,64]{1,0:T(4,128)S(1)}, s32[4,64]{1,0:T(4,128)S(1)}, u32[]{:S(2)}, u32[]{:S(2)}) collective-permute-start(s32[4,64]{1,0:T(4,128)S(1)} %pad_add_fusion.1), channel_id=1, source_target_pairs={{0,64},{64,0},{128,192},{192,128},{256,320},{320,256},{384,448},{4... | collective-permute-start | bytes 3080 | tf_op jit(solution)/shard_map/ppermute | solution.py:323
